TPU v7x, 128 devices: a whole 4x4x4 slice. The times are simulated.
128 devices in a mesh: dp: 64 (over y, x, z), tensor: 2 (over core).
Axes of the slice: x: 4, y: 4, z: 4, core: 2. Of those that a mesh axis runs over, the one named last changes fastest.
Arguments:
- tokens: bfloat16 [12288, 2048], P('dp'), may hold values from -6 to 6
- expert_ids: int32 [12288, 8], P('dp'), may hold values from 0 to 63, all different within a row
- capacity: int32 [64], replicated, may hold values from 12 to 24, as said below
- gain_attn: bfloat16 [2048], replicated, may hold values from 0.5 to 1.5
- w_qkv: bfloat16 [2048, 3, 2048], P(None, None, 'tensor'), may hold values from -0.125 to 0.125
- qk_gain: bfloat16 [2, 128], replicated, may hold values from 0.5 to 1.5
- w_out: bfloat16 [2048, 2048], P(None, 'tensor'), may hold values from -1 to 1
- gain_ffn: bfloat16 [2048], replicated, may hold values from 0.5 to 1.5
- w_router: bfloat16 [2048, 64], replicated, may hold values from -0.0625 to 0.0625
- w_gate_up: bfloat16 [64, 2048, 2, 1024], P('dp', None, None, 'tensor'), may hold values from -0.125 to 0.125
- w_down: bfloat16 [64, 1024, 2048], P('dp', 'tensor'), may hold values from -0.75 to 0.75
- cotangent: bfloat16 [12288, 2048], P('dp'), may hold values from -16 to 16
Outputs:
- output: bfloat16 [12288, 2048], P('dp')
- d_input: float32 [12288, 2048], P('dp')
- d_gain_attn: float32 [2048], P('dp')
- d_w_qkv: float32 [2048, 3, 2048], P('dp', None, 'tensor')
- d_qk_gain: float32 [2, 128], replicated
- d_w_out: float32 [2048, 2048], P('dp', 'tensor')
- d_gain_ffn: float32 [2048], P('dp')
- d_w_router: float32 [2048, 64], P('dp')
- d_w_gate_up: float32 [64, 2048, 2, 1024], P('dp', None, None, 'tensor')
- d_w_down: float32 [64, 1024, 2048], P('dp', 'tensor')
Inputs may be any that keep to these rules, and one draw needn't show every extreme that they name: `expert_ids`: each row names 8 different experts, and every expert is named by some row. At least a quarter of the experts have capacity exactly 24.
All inputs are finite; a program needn't handle non-finite values.
Results may differ from a plain program's by a relative error of at most 0.023.
Values may be sent and summed in bfloat16 or wider, within the bound.
No kernel may reach another device: no remote copies, remote signals or barrier semaphores. Data moves between devices by JAX's collectives and lax.ppermute only.
A program may use at most 256 MiB of HBM per device.

v0:
```python
import math

import jax
import jax.numpy as jnp
from jax import lax
from jax.sharding import PartitionSpec as P


def rms_scale(values):
    return lax.rsqrt(jnp.mean(values * values, axis=-1, keepdims=True) + 1e-06)


def rotary(length, half_dim):
    position = jnp.arange(length, dtype=jnp.float32)
    inverse = 50000.0 ** (-jnp.arange(half_dim, dtype=jnp.float32) / half_dim)
    angles = position[:, None] * inverse[None, :]
    return (jnp.cos(angles)[:, None, :], jnp.sin(angles)[:, None, :])


def turn(values, cosine, sine):
    half_dim = values.shape[-1] // 2
    front = values[..., :half_dim]
    behind = values[..., half_dim:]
    return jnp.concatenate(
        [front * cosine - behind * sine, behind * cosine + front * sine], axis=-1
    )


def unturn(grads, cosine, sine):
    half_dim = grads.shape[-1] // 2
    front = grads[..., :half_dim]
    behind = grads[..., half_dim:]
    return jnp.concatenate(
        [front * cosine + behind * sine, behind * cosine - front * sine], axis=-1
    )


def norm_back(grad_normed, raw, scale, gain):
    unit = raw * scale
    weighted = grad_normed * gain
    d_raw = scale * (weighted - unit * jnp.mean(weighted * unit, axis=-1, keepdims=True))
    return (d_raw, grad_normed * unit)


def head_sum(partial_value):
    return lax.psum(partial_value.astype(jnp.bfloat16), "tensor").astype(jnp.float32)


def to_owners(outgoing, owners, local_count):
    arrived = lax.all_to_all(outgoing, "dp", split_axis=0, concat_axis=0, tiled=True)
    slot_count = arrived.shape[1]
    model_width = arrived.shape[2]
    arrived = arrived.reshape(owners, local_count, slot_count, model_width).transpose(1, 0, 2, 3)
    return arrived.reshape(local_count, owners * slot_count, model_width)


def to_sources(partial_value, owners):
    local_count, rows_all, model_width = partial_value.shape
    slot_count = rows_all // owners
    summed = lax.psum(partial_value.astype(jnp.bfloat16), "tensor")
    columns = summed.shape[2]
    outgoing = summed.reshape(local_count, owners, slot_count, columns).transpose(1, 0, 2, 3)
    outgoing = outgoing.reshape(owners * local_count, slot_count, columns)
    returned = lax.all_to_all(outgoing, "dp", split_axis=0, concat_axis=0, tiled=True)
    return returned


def on_device(
    tokens,
    expert_ids,
    capacity,
    gain_attn,
    w_qkv,
    qk_gain,
    w_out,
    gain_ffn,
    w_router,
    w_gate_up,
    w_down,
    cotangent,
):
    length, model_width = tokens.shape
    top_count = expert_ids.shape[1]
    expert_count = capacity.shape[0]
    owners = lax.axis_size("dp")
    local_count = w_down.shape[0]
    slot_count = length * top_count // expert_count
    head_dim = qk_gain.shape[1]
    heads_here = w_qkv.shape[2] // head_dim
    inverse_root = 1.0 / math.sqrt(head_dim)
    residual_in = tokens.astype(jnp.float32)
    scale_one = rms_scale(residual_in)
    gain_one = gain_attn.astype(jnp.float32)
    normed_one = (residual_in * scale_one * gain_one).astype(jnp.bfloat16)
    projected = jnp.einsum("sd,dcn->scn", normed_one, w_qkv, preferred_element_type=jnp.float32)
    projected = projected.reshape(length, 3, heads_here, head_dim)
    query_raw = projected[:, 0]
    key_raw = projected[:, 1]
    value_in = projected[:, 2].astype(jnp.bfloat16)
    cosine, sine = rotary(length, head_dim // 2)
    qk_gains = qk_gain.astype(jnp.float32)
    query_scale = rms_scale(query_raw)
    key_scale = rms_scale(key_raw)
    query_in = turn(query_raw * query_scale * qk_gains[0], cosine, sine).astype(jnp.bfloat16)
    key_in = turn(key_raw * key_scale * qk_gains[1], cosine, sine).astype(jnp.bfloat16)
    scores = (
        jnp.einsum("qhd,khd->hqk", query_in, key_in, preferred_element_type=jnp.float32)
        * inverse_root
    )
    highest = jnp.max(scores, axis=-1, keepdims=True)
    log_total = highest + jnp.log(jnp.sum(jnp.exp(scores - highest), axis=-1, keepdims=True))
    weights = jnp.exp(scores - log_total).astype(jnp.bfloat16)
    attended = jnp.einsum("hqk,khd->qhd", weights, value_in, preferred_element_type=jnp.float32)
    attended = attended.astype(jnp.bfloat16).reshape(length, heads_here * head_dim)
    attn_out = head_sum(
        jnp.einsum("sn,dn->sd", attended, w_out, preferred_element_type=jnp.float32)
    )
    middle = residual_in + attn_out
    scale_two = rms_scale(middle)
    gain_two = gain_ffn.astype(jnp.float32)
    normed_two = (middle * scale_two * gain_two).astype(jnp.bfloat16)
    logits = jnp.dot(normed_two, w_router, preferred_element_type=jnp.float32)
    router_probs = jax.nn.softmax(logits, axis=-1)
    chosen = expert_ids[:, :, None] == jnp.arange(expert_count, dtype=jnp.int32)[None, None, :]
    picked = jnp.sum(jnp.where(chosen, router_probs[:, None, :], 0.0), axis=-1)
    picked_total = jnp.sum(picked, axis=-1, keepdims=True)
    gates = picked / picked_total
    flat_ids = expert_ids.reshape(-1)
    onehot = (flat_ids[:, None] == jnp.arange(expert_count, dtype=jnp.int32)[None, :]).astype(
        jnp.int32
    )
    earlier = jnp.cumsum(onehot, axis=0) - onehot
    ranks = jnp.sum(earlier * onehot, axis=1)
    limits = jnp.sum(onehot * capacity[None, :], axis=1)
    pair_count = length * top_count
    slot_index = jnp.where(ranks < limits, flat_ids * slot_count + ranks, expert_count * slot_count)
    pair_of_slot = (
        jnp.full((expert_count * slot_count,), pair_count, jnp.int32)
        .at[slot_index]
        .set(jnp.arange(pair_count, dtype=jnp.int32), mode="drop")
    )
    token_of_slot = pair_of_slot // top_count
    padded_two = jnp.concatenate([normed_two, jnp.zeros((1, model_width), jnp.bfloat16)], axis=0)
    dispatch = padded_two[token_of_slot].reshape(expert_count, slot_count, model_width)
    expert_rows = to_owners(dispatch, owners, local_count)
    gate_up = jnp.einsum(
        "erd,edcf->ercf", expert_rows, w_gate_up, preferred_element_type=jnp.float32
    )
    gate_val = gate_up[:, :, 0]
    up_val = gate_up[:, :, 1]
    sig_gate = jax.nn.sigmoid(gate_val)
    silu_gate = gate_val * sig_gate
    hidden = (silu_gate * up_val).astype(jnp.bfloat16)
    returned = to_sources(
        jnp.einsum("erf,efd->erd", hidden, w_down, preferred_element_type=jnp.float32), owners
    )
    returned_flat = jnp.concatenate(
        [returned.reshape(-1, model_width), jnp.zeros((1, model_width), jnp.bfloat16)], axis=0
    )
    per_pair = returned_flat[slot_index].reshape(length, top_count, model_width)
    mixture = jnp.sum(per_pair * gates[:, :, None], axis=1)
    output = (middle + mixture).astype(jnp.bfloat16)
    upstream = cotangent.astype(jnp.float32)
    d_gates = jnp.sum(per_pair * upstream[:, None, :], axis=-1)
    padded_grad = jnp.concatenate([upstream, jnp.zeros((1, model_width), jnp.float32)], axis=0)
    gate_pad = jnp.concatenate([gates.reshape(-1), jnp.zeros((1,), jnp.float32)])
    grad_dispatch = (padded_grad[token_of_slot] * gate_pad[pair_of_slot][:, None]).astype(
        jnp.bfloat16
    )
    grad_dispatch = grad_dispatch.reshape(expert_count, slot_count, model_width)
    d_picked = (d_gates - jnp.sum(d_gates * gates, axis=-1, keepdims=True)) / picked_total
    d_probs = jnp.sum(jnp.where(chosen, d_picked[:, :, None], 0.0), axis=1)
    d_logits = (
        router_probs * (d_probs - jnp.sum(router_probs * d_probs, axis=-1, keepdims=True))
    ).astype(jnp.bfloat16)
    grad_router = jnp.einsum("sd,se->de", normed_two, d_logits, preferred_element_type=jnp.float32)
    d_normed_two = jnp.einsum("se,de->sd", d_logits, w_router, preferred_element_type=jnp.float32)
    grad_rows = to_owners(grad_dispatch, owners, local_count)
    d_hidden = jnp.einsum("erd,efd->erf", grad_rows, w_down, preferred_element_type=jnp.float32)
    grad_down = jnp.einsum("erf,erd->efd", hidden, grad_rows, preferred_element_type=jnp.float32)
    d_gate_val = d_hidden * up_val * sig_gate * (1.0 + gate_val * (1.0 - sig_gate))
    d_up_val = d_hidden * silu_gate
    d_gate_up = jnp.stack([d_gate_val, d_up_val], axis=2).astype(jnp.bfloat16)
    grad_gate_up = jnp.einsum(
        "erd,ercf->edcf", expert_rows, d_gate_up, preferred_element_type=jnp.float32
    )
    back_rows = to_sources(
        jnp.einsum("ercf,edcf->erd", d_gate_up, w_gate_up, preferred_element_type=jnp.float32),
        owners,
    )
    back_flat = jnp.concatenate(
        [back_rows.reshape(-1, model_width), jnp.zeros((1, model_width), jnp.bfloat16)], axis=0
    )
    d_normed_two = d_normed_two + jnp.sum(
        back_flat[slot_index].reshape(length, top_count, model_width).astype(jnp.float32), axis=1
    )
    d_middle_norm, gain_terms_two = norm_back(d_normed_two, middle, scale_two, gain_two)
    d_middle = upstream + d_middle_norm
    d_attn = d_middle.astype(jnp.bfloat16)
    grad_out = jnp.einsum("sd,sn->dn", d_attn, attended, preferred_element_type=jnp.float32)
    d_attended = jnp.einsum("sd,dn->sn", d_attn, w_out, preferred_element_type=jnp.float32)
    d_attended = d_attended.astype(jnp.bfloat16).reshape(length, heads_here, head_dim)
    again = (
        jnp.einsum("qhd,khd->hqk", query_in, key_in, preferred_element_type=jnp.float32)
        * inverse_root
    )
    probs = jnp.exp(again - log_total)
    d_value = jnp.einsum(
        "hqk,qhd->khd", probs.astype(jnp.bfloat16), d_attended, preferred_element_type=jnp.float32
    )
    d_probs_att = jnp.einsum(
        "qhd,khd->hqk", d_attended, value_in, preferred_element_type=jnp.float32
    )
    d_scores = (
        probs * (d_probs_att - jnp.sum(probs * d_probs_att, axis=-1, keepdims=True))
    ).astype(jnp.bfloat16)
    d_query = unturn(
        jnp.einsum("hqk,khd->qhd", d_scores, key_in, preferred_element_type=jnp.float32)
        * inverse_root,
        cosine,
        sine,
    )
    d_key = unturn(
        jnp.einsum("hqk,qhd->khd", d_scores, query_in, preferred_element_type=jnp.float32)
        * inverse_root,
        cosine,
        sine,
    )
    d_query_raw, query_terms = norm_back(d_query, query_raw, query_scale, qk_gains[0])
    d_key_raw, key_terms = norm_back(d_key, key_raw, key_scale, qk_gains[1])
    grad_qk_local = jnp.stack([jnp.sum(query_terms, axis=(0, 1)), jnp.sum(key_terms, axis=(0, 1))])
    d_projected = jnp.stack([d_query_raw, d_key_raw, d_value], axis=1).astype(jnp.bfloat16)
    d_projected = d_projected.reshape(length, 3, heads_here * head_dim)
    grad_qkv = jnp.einsum(
        "sd,scn->dcn", normed_one, d_projected, preferred_element_type=jnp.float32
    )
    d_normed_one = head_sum(
        jnp.einsum("scn,dcn->sd", d_projected, w_qkv, preferred_element_type=jnp.float32)
    )
    d_input_norm, gain_terms_one = norm_back(d_normed_one, residual_in, scale_one, gain_one)
    grad_input = d_middle + d_input_norm
    summed = (
        lax.psum_scatter(jnp.sum(gain_terms_one, axis=0), "dp", scatter_dimension=0, tiled=True),
        lax.psum_scatter(grad_qkv, "dp", scatter_dimension=0, tiled=True),
        lax.psum_scatter(grad_out, "dp", scatter_dimension=0, tiled=True),
        lax.psum_scatter(jnp.sum(gain_terms_two, axis=0), "dp", scatter_dimension=0, tiled=True),
        lax.psum_scatter(grad_router, "dp", scatter_dimension=0, tiled=True),
    )
    grad_qk = lax.psum(grad_qk_local, ("dp", "tensor"))
    return (
        output,
        grad_input,
        summed[0],
        summed[1],
        grad_qk,
        summed[2],
        summed[3],
        summed[4],
        grad_gate_up,
        grad_down,
    )


def solution(mesh):
    return jax.shard_map(
        on_device,
        mesh=mesh,
        in_specs=(
            P("dp", None),
            P("dp", None),
            P(),
            P(),
            P(None, None, "tensor"),
            P(),
            P(None, "tensor"),
            P(),
            P(),
            P("dp", None, None, "tensor"),
            P("dp", "tensor", None),
            P("dp", None),
        ),
        out_specs=(
            P("dp", None),
            P("dp", None),
            P("dp"),
            P("dp", None, "tensor"),
            P(),
            P("dp", "tensor"),
            P("dp"),
            P("dp", None),
            P("dp", None, None, "tensor"),
            P("dp", "tensor", None),
        ),
        check_vma=False,
    )
```

profile of v0, /device:TPU:0, one launch (start us, length us, event | category | flops | bytes accessed | tf_op | source)
XLA Modules:
  0.0 1735.1 jit_solution(8059936466669236868)
XLA Ops:
  7.3 1.6 fusion.27
  8.8 0.7 convert_element_type.123
  9.5 6.1 fusion.53
  21.1 0.9 copy-done.4
  23.1 0.7 copy-done.32
  23.8 2.4 convolution_convert_fusion.1
  26.8 0.8 fusion.50
  27.7 31.5 %reduce-window.6 = s32[64,12,128]{2,1,0:T(8,128)S(1)} reduce-window(s32[64,12,128]{2,1,0:T(8,128)} %fusion.50, s32[]{:T(128)} %constant.57.clone.1), window={size=1x1x128 pad=0_0x0_0x127_0}, to_apply=%region_7.0 | reduce-window | flops 12484608 | bytes 786436 | tf_op jit(solution)/shard_map/reduce-window
  59.2 1.0 slice.88
  60.2 1.3 copy.108
  62.1 6.2 scatter_custom_fusion
  68.4 1.5 multiply_reduce_fusion.3
  70.3 0.9 copy-done.14
  71.3 7.0 gather_fusion
  78.3 11.9 all-to-all-start
  90.2 1.4 concatenate.66
  91.6 14.0 gather_fusion.2
  106.4 8.4 gather_fusion.3
  114.9 7.9 multiply_convert_fusion
  122.8 49.2 %all-to-all-done = bf16[64,24,2048]{2,1,0:T(8,128)(2,1)} async-done(((bf16[64,24,2048]{2,1,0:T(8,128)(2,1)}), bf16[64,24,2048]{2,1,0:T(8,128)(2,1)}, u32[]{:S(2)}, u32[]{:S(2)}) %all-to-all-start) | async-done | bytes 6291488 | tf_op jit(solution)/shard_map/all_to_all | solution.py:50
  172.0 10.1 all-to-all-start.2
  182.2 10.0 convolution_bitcast_fusion.1
  192.2 2.7 copy-done.21
  194.9 1.1 multiply_convert_fusion.1
  196.0 1.2 copy-done.36
  197.1 5.4 convolution_convert_fusion
  202.5 60.6 %all-to-all-done.2 = bf16[64,24,2048]{2,1,0:T(8,128)(2,1)} async-done(((bf16[64,24,2048]{2,1,0:T(8,128)(2,1)}), bf16[64,24,2048]{2,1,0:T(8,128)(2,1)}, u32[]{:S(2)}, u32[]{:S(2)}) %all-to-all-start.2) | async-done | bytes 6291488 | tf_op jit(solution)/shard_map/all_to_all | solution.py:50
  263.1 8.6 fusion.31
  271.7 8.9 bitcast_convert_fusion
  280.6 60.8 %all-reduce.16.cloned.1.call-done = (bf16[64,24,2048]{2,1,0:T(8,128)(2,1)}, bf16[64,24,2048]{2,1,0:T(8,128)(2,1)}) async-done(((bf16[64,24,2048]{2,1,0:T(8,128)(2,1)}, bf16[64,24,2048]{2,1,0:T(8,128)(2,1)}), (bf16[64,24,2048]{2,1,0:T(8,128)(2,1)}, bf16[64,24,2048]{2,1,0:T(8,128)(2,1)})) %all-reduce.16.cloned.1.call-update) | async-done | bytes 12582928 | tf_op jit(solution)/shard_map/psum | solution.py:60
  341.5 85.5 %all_to_all.20 = bf16[64,24,2048]{2,1,0:T(8,128)(2,1)} all-to-all(bf16[64,24,2048]{2,1,0:T(8,128)(2,1)} %get-tuple-element.79), channel_id=1, replica_groups=mesh['dp'=64,'tensor'=2] {'dp'}, dimensions={0} | all-to-all | bytes 12582912 | tf_op jit(solution)/shard_map/all_to_all | solution.py:64
  427.0 6.5 all-to-all-start.1
  433.5 1.3 convert_element_type.143
  434.9 6.6 concatenate.68
  441.5 25.4 %gather_fusion.4 = bf16[1536,2048]{1,0:T(8,128)(2,1)} fusion(bf16[1537,2048]{1,0:T(8,128)(2,1)} %concatenate.68, s32[2048]{0:T(1024)S(1)} %pad_clamp_fusion.1), kind=kCustom, calls=%fused_computation.4 | custom fusion | bytes 12589056 | tf_op jit(solution)/shard_map/gather | solution.py:195
  466.9 8.9 convert_reduce_fusion
  475.7 40.6 %all-to-all-done.1 = bf16[64,24,2048]{2,1,0:T(8,128)(2,1)} async-done(((bf16[64,24,2048]{2,1,0:T(8,128)(2,1)}), bf16[64,24,2048]{2,1,0:T(8,128)(2,1)}, u32[]{:S(2)}, u32[]{:S(2)}) %all-to-all-start.1) | async-done | bytes 6291488 | tf_op jit(solution)/shard_map/all_to_all | solution.py:64
  516.4 6.6 concatenate.65
  523.0 16.3 gather_fusion.1
  539.3 8.3 fusion.1
  547.9 2.3 multiply_reduce_fusion
  550.3 1.7 multiply_add_fusion
  551.9 0.8 copy-done.13
  552.7 1.0 fusion.36
  557.8 1.5 fusion.34
  559.8 2.0 multiply_add_fusion.1
  561.9 0.8 multiply_reduce_fusion.4
  563.0 0.8 multiply_reduce_fusion.5
  563.8 0.7 bitcast_dynamic-update-slice_fusion.1
  565.2 1.0 copy-done.34
  566.3 9.7 fusion.13
  576.1 2.7 fusion.97
  579.1 4.5 fusion.59
  583.7 1.2 copy-done.35
  584.9 10.2 fusion.51
  596.9 9.8 convolution_bitcast_fusion
  606.7 16.5 copy.124
  623.2 7.8 convolution_bitcast_fusion.2
  631.0 66.4 %psum.39 = f32[2,128]{1,0:T(2,128)} all-reduce(f32[2,128]{1,0:T(2,128)S(1)} %pad_maximum_fusion.12), channel_id=1, replica_groups=mesh['dp'=64,'tensor'=2] {'dp','tensor'}, use_global_device_ids=true, to_apply=%region_35.36 | all-reduce | flops 256 | bytes 2048 | tf_op jit(solution)/shard_map/psum | solution.py:249
  697.5 1.8 fusion.26
  699.3 345.0 %all-reduce.6 = (f32[2048]{0:T(1024)S(1)}, f32[2048]{0:T(1024)S(1)}) all-reduce(f32[2048]{0:T(1024)S(1)} %get-tuple-element.68, f32[2048]{0:T(1024)S(1)} %get-tuple-element.62), channel_id=2, replica_groups=mesh['dp'=64,'tensor'=2] {'dp'}, use_global_device_ids=true, to_apply=%region_31.32.clone | all-reduce | flops 4096 | bytes 32768
  1045.4 3.3 fusion.23
  1048.8 274.9 %reduce-scatter.6.cloned.1.call-done = f32[32,1024]{1,0:T(8,128)} async-done(((f32[2048,1024]{1,0:T(8,128)}), f32[32,1024]{1,0:T(8,128)}) %reduce-scatter.6.cloned.1.call-update) | async-done | bytes 131088 | tf_op jit(solution)/shard_map/reduce_scatter | solution.py:245
  1323.6 404.5 %reduce-scatter.4.cloned.1.call-done = f32[32,3,1024]{2,0,1:T(8,128)} async-done(((f32[2048,3,1024]{2,0,1:T(8,128)}), f32[32,3,1024]{2,0,1:T(8,128)}) %reduce-scatter.4.cloned.1.call-update) | async-done | bytes 393232 | tf_op jit(solution)/shard_map/reduce_scatter | solution.py:244
  (216 shorter events, 17.6 us)
Async XLA Ops:
  7.2 190.0 %copy-start = (bf16[1,512,2048]{2,1,0:T(8,128)(2,1)S(1)}, bf16[1,512,2048]{2,1,0:T(8,128)(2,1)}, u32[]{:S(2)}) copy-start(bf16[1,512,2048]{2,1,0:T(8,128)(2,1)} %param.22) | copy-start | bytes 6291460
  7.2 2.3 copy-start.2
  7.2 61.2 %all-reduce.12.cloned.1.call-start = ((), (), s32[]{:S(2)}) async-start(), calls=%async_computation.7 | async-start | bytes 1572864 | tf_op jit(solution)/shard_map/psum | solution.py:46
  8.8 6.8 copy-start.54
  9.5 6.1 copy-start.43
  16.2 4.8 copy-start.30
  16.9 1.4 copy-start.10
  16.9 1.7 copy-start.8
  16.9 1.4 copy-start.60
  16.9 1.7 copy-start.58
  17.3 1.6 copy-start.39
  17.3 1.6 copy-start.41
  19.6 1.2 copy-start.28
  19.6 4.2 copy-start.12
  20.8 1.2 copy-start.4
  23.8 2.4 copy-start.53
  23.8 2.8 copy-start.62
  26.6 43.4 %copy-start.51 = (f32[2048]{0:T(1024)}, f32[2048]{0:T(1024)S(1)}, u32[]{:S(2)}) copy-start(f32[2048]{0:T(1024)S(1)} %convert_element_type.132) | copy-start | bytes 24580
  59.2 2.6 copy-start.63
  68.4 1.6 copy-start.16
  70.0 1.3 copy-start.56
  78.3 11.9 copy-start.18
  78.3 93.7 %all-to-all-start = ((bf16[64,24,2048]{2,1,0:T(8,128)(2,1)}), bf16[64,24,2048]{2,1,0:T(8,128)(2,1)}, u32[]{:S(2)}, u32[]{:S(2)}) async-start(bf16[64,24,2048]{2,1,0:T(8,128)(2,1)} %bitcast.208), calls=%async_computation | async-start | bytes 12582912 | tf_op jit(solution)/shard_map/all_to_all | solution.py:50
  91.5 14.0 copy-start.15
  91.5 14.0 copy-start.38
  172.0 91.0 %all-to-all-start.2 = ((bf16[64,24,2048]{2,1,0:T(8,128)(2,1)}), bf16[64,24,2048]{2,1,0:T(8,128)(2,1)}, u32[]{:S(2)}, u32[]{:S(2)}) async-start(bf16[64,24,2048]{2,1,0:T(8,128)(2,1)} %multiply_convert_fusion), calls=%async_computation.2 | async-start | bytes 12582912 | tf_op jit(solution)/shard_map/all_to_all | solution.py:50
  182.1 159.3 %all-reduce.16.cloned.1.call-start = ((), (), s32[]{:S(2)}) async-start(), calls=%async_computation.12 | async-start | bytes 25165824 | tf_op jit(solution)/shard_map/psum | solution.py:60
  192.2 2.7 copy-start.21
  196.0 1.2 copy-start.36
  263.1 8.6 copy-start.64
  271.7 8.9 copy-start.67
  271.7 8.9 copy-start.69
  427.0 6.6 copy-start.19
  427.0 89.4 %all-to-all-start.1 = ((bf16[64,24,2048]{2,1,0:T(8,128)(2,1)}), bf16[64,24,2048]{2,1,0:T(8,128)(2,1)}, u32[]{:S(2)}, u32[]{:S(2)}) async-start(bf16[64,24,2048]{2,1,0:T(8,128)(2,1)} %get-tuple-element.78), calls=%async_computation.1 | async-start | bytes 12582912 | tf_op jit(solution)/shard_map/all_to_all | solution.py:64
  433.5 264.0 %all-reduce.14.cloned.1.call-start = ((), (), s32[]{:S(2)}) async-start(), calls=%async_computation.8 | async-start | bytes 1572864 | tf_op jit(solution)/shard_map/psum | solution.py:46
  539.3 8.6 copy-start.3
  539.3 8.6 copy-start.17
  539.3 8.6 copy-start.52
  539.3 8.6 copy-start.57
  547.9 2.3 copy-start.20
  550.2 2.5 copy-start.13
  551.9 1.8 copy-start.6
  552.7 1.4 copy-start.5
  552.7 1.4 copy-start.46
  556.7 1.1 copy-start.25
  557.8 2.0 copy-start.40
  557.8 2.0 copy-start.42
  559.8 2.1 copy-start.9
  559.8 2.1 copy-start.48
  559.8 2.1 copy-start.59
  561.9 1.1 copy-start.11
  561.9 1.1 copy-start.50
  561.9 1.1 copy-start.61
  576.0 3.1 copy-start.7
  576.0 3.1 copy-start.33
  576.0 472.7 %reduce-scatter.8.cloned.1.call-start = ((), (), s32[]{:S(2)}) async-start(), calls=%async_computation.11 | async-start | bytes 1064960 | tf_op jit(solution)/shard_map/reduce_scatter | solution.py:247
  578.9 744.8 %reduce-scatter.6.cloned.1.call-start = ((), (), s32[]{:S(2)}) async-start(), calls=%async_computation.10 | async-start | bytes 8519680 | tf_op jit(solution)/shard_map/reduce_scatter | solution.py:245
  583.6 1.3 copy-start.35
  583.6 1.3 copy-start.44
  583.6 1.3 copy-start.55
  583.6 1144.5 %reduce-scatter.4.cloned.1.call-start = ((), (), s32[]{:S(2)}) async-start(), calls=%async_computation.9 | async-start | bytes 25559040 | tf_op jit(solution)/shard_map/reduce_scatter | solution.py:244
  595.0 1.9 copy-start.68
  606.7 16.5 copy-start.37
  1045.4 682.7 %copy-start.1 = (bf16[1,512,2048]{2,1,0:T(8,128)(2,1)S(1)}, bf16[1,512,2048]{2,1,0:T(8,128)(2,1)}, u32[]{:S(2)}) copy-start(bf16[1,512,2048]{2,1,0:T(8,128)(2,1)} %param.22) | copy-start | bytes 6291460
  (15 other events, 12.8 us)
Sparse Core Ops, SparseCore 0:
  26.4 27.2 all-reduce.11
  280.8 60.6 all-reduce.15
  576.1 25.2 all-reduce.13
  604.2 353.5 reduce-scatter.7
  960.7 362.9 reduce-scatter.5
  1326.6 401.4 reduce-scatter.3
where the time goes:
time: 1750 us; the launch traced here: 1740 us
  waiting for transfers between devices  891 us (51%)
  blocking collectives  497 us (28%)
  local copies, waits for them, and re-layouts  129 us (7%)
  matrix products  93.6 us (5%)
  other arithmetic  79.6 us (5%)
  starting transfers between devices  28.9 us (2%)
    reduce_scatter x1, waiting for transfers between devices, on_device(): lax.psum_scatter(grad_qkv, 'dp', scatter_dimension=0, tiled=True)  404 us
    unnamed x1, blocking collectives  345 us
    reduce_scatter x1, waiting for transfers between devices, on_device(): lax.psum_scatter(grad_out, 'dp', scatter_dimension=0, tiled=True)  275 us
    all_to_all x2, waiting for transfers between devices, to_owners(): lax.all_to_all(outgoing, 'dp', split_axis=0, concat_axis=0, tiled=True)  110 us
    all_to_all x1, blocking collectives, to_sources(): lax.all_to_all(outgoing, 'dp', split_axis=0, concat_axis=0, tiled=True)  85.5 us
    psum x1, blocking collectives, on_device(): grad_qk = lax.psum(grad_qk_local, ('dp', 'tensor'))  66.4 us
    psum x1, waiting for transfers between devices, to_sources(): summed = lax.psum(partial_value.astype(jnp.bfloat16), 'tensor')  60.8 us
    all_to_all x1, waiting for transfers between devices, to_sources(): lax.all_to_all(outgoing, 'dp', split_axis=0, concat_axis=0, tiled=True)  40.6 us
  transfers between devices with their start and end apart: 9, of which 6 were waited for; matrix products, arithmetic and copies ran while one was open for 11% of the time, Pallas kernels for 0%

commit v1 on v0

v1 whole, which is shorter than its diff:
```python
import math

import jax
import jax.numpy as jnp
import numpy as np
from jax import lax
from jax.sharding import Mesh
from jax.sharding import PartitionSpec as P

AXES = ("y", "x", "z")
SIDE = 4
BF = jnp.bfloat16
F32 = jnp.float32


def dot(a, b, dims):
    return lax.dot_general(a, b, (dims, ((), ())), preferred_element_type=F32)


def rms_scale(values):
    return lax.rsqrt(jnp.mean(values * values, axis=-1, keepdims=True) + 1e-06)


def rotary(length, half_dim):
    position = np.arange(length, dtype=np.float32)
    inverse = np.float32(50000.0) ** (-np.arange(half_dim, dtype=np.float32) / np.float32(half_dim))
    angles = position[:, None] * inverse[None, :].astype(np.float32)
    return (
        jnp.asarray(np.cos(angles)[:, None, :], F32),
        jnp.asarray(np.sin(angles)[:, None, :], F32),
    )


def turn(values, cosine, sine):
    half_dim = values.shape[-1] // 2
    front = values[..., :half_dim]
    behind = values[..., half_dim:]
    return jnp.concatenate(
        [front * cosine - behind * sine, behind * cosine + front * sine], axis=-1
    )


def unturn(grads, cosine, sine):
    half_dim = grads.shape[-1] // 2
    front = grads[..., :half_dim]
    behind = grads[..., half_dim:]
    return jnp.concatenate(
        [front * cosine + behind * sine, behind * cosine - front * sine], axis=-1
    )


def norm_back(grad_normed, raw, scale, gain):
    unit = raw * scale
    weighted = grad_normed * gain
    d_raw = scale * (weighted - unit * jnp.mean(weighted * unit, axis=-1, keepdims=True))
    return (d_raw, grad_normed * unit)


def swap(value):
    return lax.ppermute(value, "tensor", [(0, 1), (1, 0)])


def shift(value, axis, step):
    return lax.ppermute(value, axis, [(i, (i + step) % SIDE) for i in range(SIDE)])


def side_by_side(own, peer, core):
    return jnp.where(
        core == 0,
        jnp.concatenate([own, peer], axis=-1),
        jnp.concatenate([peer, own], axis=-1),
    )


def block_at(value, index, dim):
    return lax.dynamic_index_in_dim(value, index, dim, keepdims=False)


def scatter_sum(value, axis, dim):
    here = lax.axis_index(axis)
    total = block_at(value, here, dim).astype(F32)
    for step in (1, 3, 2):
        sent = block_at(value, (here + step) % SIDE, dim)
        total = total + shift(sent, axis, step).astype(F32)
    return total


def all_sum(value, axis):
    here = lax.axis_index(axis)
    parts = [value] + [shift(value, axis, step) for step in (1, 2, 3)]
    stacked = jnp.stack(parts + parts)
    ordered = [block_at(stacked, (here - source) % SIDE, 0) for source in range(SIDE)]
    return (ordered[0] + ordered[1]) + (ordered[2] + ordered[3])


def exchange(value):
    return lax.all_to_all(value, AXES, split_axis=0, concat_axis=0, tiled=True)


def on_device(
    tokens,
    expert_ids,
    capacity,
    gain_attn,
    w_qkv,
    qk_gain,
    w_out,
    gain_ffn,
    w_router,
    w_gate_up,
    w_down,
    cotangent,
):
    length, width = tokens.shape
    expert_count = capacity.shape[0]
    slot_count = length * expert_ids.shape[1] // expert_count
    slots = expert_count * slot_count
    head_dim = qk_gain.shape[1]
    heads = w_qkv.shape[2] // head_dim
    inner = heads * head_dim
    hidden_here = w_down.shape[1]
    half = width // 2
    inverse_root = 1.0 / math.sqrt(head_dim)
    core = lax.axis_index("tensor")
    place = [lax.axis_index(a) for a in AXES]
    dp_index = (place[0] * SIDE + place[1]) * SIDE + place[2]

    def own_half(value):
        return lax.dynamic_slice_in_dim(value, core * half, half, axis=-1)

    experts = jnp.arange(expert_count, dtype=jnp.int32)
    member = jnp.sum((expert_ids[:, :, None] == experts).astype(F32), axis=1)
    earlier = jnp.asarray(np.tril(np.ones((length, length), np.float32), -1), BF)
    ranks = dot(earlier, member.astype(BF), ((1,), (0,)))
    kept = (member > 0.5) & (ranks < capacity.astype(F32)[None, :])
    code = jnp.where(kept, ranks, -1.0).T
    slot_hit = code[:, None, :] == jnp.arange(slot_count, dtype=jnp.int32).astype(F32)[None, :, None]
    select = slot_hit.astype(BF).reshape(slots, length)

    def dispatch(value):
        rows = dot(select, value, ((1,), (0,))).astype(BF)
        return exchange(rows.reshape(expert_count, slot_count, half)).reshape(slots, half)

    grad_own = dispatch(own_half(cotangent))

    residual_in = tokens.astype(F32)
    scale_one = rms_scale(residual_in)
    gain_one = gain_attn.astype(F32)
    normed_one = (residual_in * scale_one * gain_one).astype(BF)
    projected = jnp.einsum("sd,dcn->csn", normed_one, w_qkv, preferred_element_type=F32)
    projected = projected.reshape(3, length, heads, head_dim)
    query_raw = projected[0]
    key_raw = projected[1]
    value_in = projected[2].astype(BF)
    cosine, sine = rotary(length, head_dim // 2)
    qk_gains = qk_gain.astype(F32)
    query_scale = rms_scale(query_raw)
    key_scale = rms_scale(key_raw)
    query_in = turn(query_raw * query_scale * qk_gains[0], cosine, sine).astype(BF)
    key_in = turn(key_raw * key_scale * qk_gains[1], cosine, sine).astype(BF)
    scores = (
        jnp.einsum("qhd,khd->hqk", query_in, key_in, preferred_element_type=F32) * inverse_root
    )
    highest = jnp.max(scores, axis=-1, keepdims=True)
    raised = jnp.exp(scores - highest)
    probs_att = raised / jnp.sum(raised, axis=-1, keepdims=True)
    weights = probs_att.astype(BF)
    attended = jnp.einsum("hqk,khd->qhd", weights, value_in, preferred_element_type=F32)
    attended = attended.astype(BF).reshape(length, inner)
    partial_out = dot(attended, w_out, ((1,), (1,))).astype(BF)
    attn_out = partial_out.astype(F32) + swap(partial_out).astype(F32)
    middle = residual_in + attn_out
    scale_two = rms_scale(middle)
    gain_two = gain_ffn.astype(F32)
    normed_two = (middle * scale_two * gain_two).astype(BF)

    rows_own = dispatch(own_half(normed_two))

    logits = dot(normed_two, w_router, ((1,), (0,)))
    router_probs = jax.nn.softmax(logits, axis=-1)
    picked = router_probs * member
    picked_total = jnp.sum(picked, axis=-1, keepdims=True)
    gates = picked / picked_total
    gates_col = gates.T[:, None, :]
    slot_gates = jnp.sum(jnp.where(slot_hit, gates_col, 0.0), axis=-1)
    slot_gates = jnp.pad(slot_gates, ((0, 0), (0, 128 - slot_count)))
    slot_gates = jnp.broadcast_to(slot_gates[:, None, :], (expert_count, 8, 128))
    slot_gates = exchange(slot_gates)[:, 0, :slot_count].reshape(slots, 1)
    combine = jnp.where(slot_hit, gates_col, 0.0).astype(BF).reshape(slots, length)

    grad_rows = side_by_side(grad_own, swap(grad_own), core)
    down = w_down[0]
    pair = w_gate_up[0]
    d_hidden = dot(grad_rows, down, ((1,), (1,)))
    expert_rows = side_by_side(rows_own, swap(rows_own), core)
    gate_up = jnp.einsum("rd,dcf->rcf", expert_rows, pair, preferred_element_type=F32)
    gate_val = gate_up[:, 0]
    up_val = gate_up[:, 1]
    sig_gate = jax.nn.sigmoid(gate_val)
    silu_gate = gate_val * sig_gate
    acted = silu_gate * up_val
    hidden = acted.astype(BF)
    slot_grads = jnp.sum(d_hidden * hidden.astype(F32), axis=-1).reshape(expert_count, slot_count)
    slot_grads = jnp.pad(slot_grads, ((0, 0), (0, 128 - slot_count)))
    slot_grads = jnp.broadcast_to(slot_grads[:, None, :], (expert_count, 8, 128))
    slot_grads = exchange(slot_grads)[:, 0, :slot_count]
    d_gate_val = d_hidden * up_val * sig_gate * (1.0 + gate_val * (1.0 - sig_gate))
    d_up_val = d_hidden * silu_gate
    d_pair = jnp.stack([d_gate_val, d_up_val], axis=1)
    d_pair_low = d_pair.astype(BF)

    def to_sources(full):
        peer_first = lax.dynamic_slice_in_dim(full, (1 - core) * half, half, axis=1)
        own = lax.dynamic_slice_in_dim(full, core * half, half, axis=1)
        total = (own + swap(peer_first.astype(BF)).astype(F32)).astype(BF)
        return exchange(total.reshape(expert_count, slot_count, half)).reshape(slots, half)

    back_own = to_sources(
        jnp.einsum("rcf,dcf->rd", d_pair_low, pair, preferred_element_type=F32)
    )
    returned_own = to_sources(dot(hidden, down, ((1,), (0,))))

    gated_pair = (d_pair * slot_gates[:, :, None]).astype(BF)
    grad_gate_up = jnp.einsum("rd,rcf->dcf", expert_rows, gated_pair, preferred_element_type=F32)
    gated_hidden = (acted * slot_gates).astype(BF)
    grad_down = dot(gated_hidden, grad_rows, ((0,), (0,)))

    spread = jnp.sum(jnp.where(slot_hit, slot_grads[:, :, None], 0.0), axis=1).T
    d_gates = spread + swap(spread)
    d_picked = member * (d_gates - jnp.sum(d_gates * gates, axis=-1, keepdims=True)) / picked_total
    d_logits = (
        router_probs * (d_picked - jnp.sum(router_probs * d_picked, axis=-1, keepdims=True))
    ).astype(BF)
    grad_router = dot(normed_two, d_logits, ((0,), (0,)))

    mix_own = dot(combine, returned_own, ((0,), (0,)))
    out_own = (own_half(middle) + mix_own).astype(BF)
    output = side_by_side(out_own, swap(out_own), core)

    d_two_own = dot(combine, back_own, ((0,), (0,)))
    d_two_own = side_by_side(d_two_own, swap(d_two_own), core)
    d_normed_two = d_two_own + dot(d_logits, w_router, ((1,), (1,)))

    upstream = cotangent.astype(F32)
    d_middle_norm, gain_terms_two = norm_back(d_normed_two, middle, scale_two, gain_two)
    d_middle = upstream + d_middle_norm
    d_attn = d_middle.astype(BF)
    gain_two_local = jnp.sum(gain_terms_two, axis=0)

    grad_out = dot(d_attn, attended, ((0,), (0,))).astype(BF)
    d_attended = dot(d_attn, w_out, ((1,), (0,))).astype(BF).reshape(length, heads, head_dim)
    d_value = jnp.einsum("hqk,qhd->khd", weights, d_attended, preferred_element_type=F32)
    d_probs_att = jnp.einsum("qhd,khd->hqk", d_attended, value_in, preferred_element_type=F32)
    d_scores = (
        probs_att * (d_probs_att - jnp.sum(probs_att * d_probs_att, axis=-1, keepdims=True))
    ).astype(BF)
    d_query = unturn(
        jnp.einsum("hqk,khd->qhd", d_scores, key_in, preferred_element_type=F32) * inverse_root,
        cosine,
        sine,
    )
    d_key = unturn(
        jnp.einsum("hqk,qhd->khd", d_scores, query_in, preferred_element_type=F32) * inverse_root,
        cosine,
        sine,
    )
    d_query_raw, query_terms = norm_back(d_query, query_raw, query_scale, qk_gains[0])
    d_key_raw, key_terms = norm_back(d_key, key_raw, key_scale, qk_gains[1])
    grad_qk = jnp.stack([jnp.sum(query_terms, axis=(0, 1)), jnp.sum(key_terms, axis=(0, 1))])
    d_parts = [
        g.astype(BF).reshape(length, inner) for g in (d_query_raw, d_key_raw, d_value)
    ]

    packed = jnp.concatenate(
        [
            grad_router.reshape(SIDE**3, -1),
            gain_two_local.reshape(SIDE**3, -1),
            jnp.zeros((SIDE**3, 96), F32),
        ],
        axis=1,
    )
    columns = packed.shape[1]
    packed = exchange(packed.reshape(SIDE**3, columns // 128, 128))
    packed = jnp.sum(packed, axis=0).reshape(columns)
    router_rows = width // SIDE**3
    grad_router_out = packed[: router_rows * expert_count].reshape(router_rows, expert_count)
    grad_gain_two = packed[router_rows * expert_count : router_rows * (expert_count + 1)]

    grid = (SIDE, SIDE, SIDE, router_rows)
    cuts = (0, 384, 768, inner)
    orders = ((1, 2, 0), (2, 0, 1), (0, 1, 2))
    pieces = []
    for part, order in enumerate(orders):
        value = grad_out[:, cuts[part] : cuts[part + 1]].reshape(*grid, -1)
        names = [0, 1, 2]
        for axis in order:
            dim = names.index(axis)
            value = scatter_sum(value, AXES[axis], dim)
            names.remove(axis)
            if names:
                value = value.astype(BF)
        pieces.append(value)
    grad_out_here = jnp.concatenate(pieces, axis=1)

    grouped = normed_one.reshape(length, SIDE, SIDE, SIDE, router_rows)
    pieces = []
    for part, (group, second, third) in enumerate(((0, 1, 2), (1, 2, 0), (2, 0, 1))):
        here = place[group]
        total = None
        for step in (0, 1, 3, 2):
            left = block_at(grouped, (here + step) % SIDE, 1 + group).reshape(length, width // SIDE)
            right = d_parts[part]
            if step:
                left = shift(left, AXES[group], step)
                right = shift(right, AXES[group], step)
            product = dot(left, right, ((0,), (0,)))
            total = product if total is None else total + product
        value = total.astype(BF).reshape(SIDE, SIDE, router_rows, inner)
        names = [a for a in (0, 1, 2) if a != group]
        value = scatter_sum(value, AXES[second], names.index(second)).astype(BF)
        value = scatter_sum(value, AXES[third], 0)
        pieces.append(value)
    grad_qkv = jnp.stack(pieces, axis=1)
    rows_here = lax.dynamic_slice_in_dim(w_qkv, dp_index * router_rows, router_rows, axis=0)
    gain_here = lax.dynamic_slice_in_dim(gain_one, dp_index * router_rows, router_rows, axis=0)
    grad_gain_one = jnp.sum(grad_qkv * rows_here.astype(F32), axis=(1, 2))
    grad_gain_one = (grad_gain_one + swap(grad_gain_one)) / gain_here

    d_one = jnp.zeros((length, width), F32)
    for part in range(3):
        d_one = d_one + dot(d_parts[part], w_qkv[:, part], ((1,), (1,)))
    d_one = d_one.astype(BF)
    d_one = d_one.astype(F32) + swap(d_one).astype(F32)
    d_input_norm, _ = norm_back(d_one, residual_in, scale_one, gain_one)
    grad_input = d_middle + d_input_norm

    grad_qk = grad_qk + swap(grad_qk)
    for axis in AXES:
        grad_qk = all_sum(grad_qk, axis)

    return (
        output,
        grad_input,
        grad_gain_one,
        grad_qkv,
        grad_qk,
        grad_out_here,
        grad_gain_two,
        grad_router_out,
        grad_gate_up[None],
        grad_down[None],
    )


def solution(mesh):
    names = AXES + ("tensor",)
    torus = Mesh(mesh.devices.reshape(SIDE, SIDE, SIDE, 2), names)
    return jax.shard_map(
        on_device,
        mesh=torus,
        in_specs=(
            P(AXES, None),
            P(AXES, None),
            P(),
            P(),
            P(None, None, "tensor"),
            P(),
            P(None, "tensor"),
            P(),
            P(),
            P(AXES, None, None, "tensor"),
            P(AXES, "tensor", None),
            P(AXES, None),
        ),
        out_specs=(
            P(AXES, None),
            P(AXES, None),
            P(AXES),
            P(AXES, None, "tensor"),
            P(),
            P(AXES, "tensor"),
            P(AXES),
            P(AXES, None),
            P(AXES, None, None, "tensor"),
            P(AXES, "tensor", None),
        ),
        check_vma=False,
    )
```

time: 1750 us -> 627 us (0.36)
  waiting for transfers between devices: 891 us -> 198 us
  blocking collectives: 497 us -> 0 us
  starting transfers between devices: 28.9 us -> 166 us
  local copies, waits for them, and re-layouts: 129 us -> 73.4 us
  matrix products: 93.6 us -> 127 us
  other arithmetic: 79.6 us -> 48.9 us
    reduce_scatter x3 -> x0, waiting for transfers between devices: 679 us -> none  [the longest x1 404 us: on_device(): lax.psum_scatter(grad_qkv, 'dp', scatter_dimension=0, tiled=True)]
    unnamed x1 -> x0, blocking collectives: 345 us -> none
    ppermute x0 -> x83, starting transfers between devices: none -> 107 us  [the longest x72 105 us: shift(): lax.ppermute(value, axis, [(i, (i + step) % SIDE) for i in range(SIDE)])]
    all_to_all x1 -> x0, blocking collectives: 85.5 us -> none  [to_sources(): lax.all_to_all(outgoing, 'dp', split_axis=0, concat_axis=0, tiled=True)]
    ppermute x0 -> x83, waiting for transfers between devices: none -> 73.8 us  [the longest x72 71.8 us: shift(): lax.ppermute(value, axis, [(i, (i + step) % SIDE) for i in range(SIDE)])]
    gather x5 -> x0, local copies, waits for them, and re-layouts: 71.1 us -> none  [the longest x1 25.4 us: on_device(): back_flat[slot_index].reshape(length, top_count, model_width)]
    psum x1 -> x0, blocking collectives: 66.4 us -> none  [on_device(): grad_qk = lax.psum(grad_qk_local, ('dp', 'tensor'))]
    psum x3 -> x0, waiting for transfers between devices: 60.9 us -> none  [the longest x1 60.8 us: to_sources(): summed = lax.psum(partial_value.astype(jnp.bfloat16), 'tensor')]
  transfers between devices with their start and end apart: 9 -> 90, of which waited for: 6 -> 35; matrix products, arithmetic and copies ran while one was open for 11% -> 28% of each run, Pallas kernels for 0% -> 0%
where the time goes in v1:
time: 627 us; the launch traced here: 616 us
  waiting for transfers between devices  198 us (32%)
  starting transfers between devices  166 us (26%)
  matrix products  127 us (20%)
  local copies, waits for them, and re-layouts  73.4 us (12%)
  other arithmetic  48.9 us (8%)
    all_to_all x7, waiting for transfers between devices, exchange(): return lax.all_to_all(value, AXES, split_axis=0, concat_axis=0, tiled=True)  124 us
    ppermute x72, starting transfers between devices, shift(): lax.ppermute(value, axis, [(i, (i + step) % SIDE) for i in range(SIDE)])  105 us
    ppermute x72, waiting for transfers between devices, shift(): lax.ppermute(value, axis, [(i, (i + step) % SIDE) for i in range(SIDE)])  71.8 us
    dot_general x29, matrix products, dot(): return lax.dot_general(a, b, (dims, ((), ())), preferred_element_type=F32)  70.8 us
    all_to_all x7, starting transfers between devices, exchange(): return lax.all_to_all(value, AXES, split_axis=0, concat_axis=0, tiled=True)  59.3 us
    unnamed x226, local copies, waits for them, and re-layouts  40.1 us
    dot_general x1, matrix products, on_device(): jnp.einsum('rd,rcf->dcf', expert_rows, gated_pair, preferred_element_type...  16.7 us
    dot_general x1, matrix products, on_device(): jnp.einsum('rd,dcf->rcf', expert_rows, pair, preferred_element_type=F32)  13.9 us
  transfers between devices with their start and end apart: 90, of which 35 were waited for; matrix products, arithmetic and copies ran while one was open for 28% of the time, Pallas kernels for 0%

profile of v1, /device:TPU:0, one launch (start us, length us, event | category | flops | bytes accessed | tf_op | source)
XLA Modules:
  0.0 616.1 jit_solution(12035466184048467521)
XLA Ops:
  4.9 6.3 %convolution_bitcast_fusion.3 = f32[3,192,1024]{2,1,0:T(8,128)S(1)} fusion(bf16[2048,3,1024]{2,0,1:T(8,128)(2,1)} %param.19, bf16[192,2048]{1,0:T(8,128)(2,1)S(1)} %fusion.44), kind=kOutput, calls=%fused_computation.66 | convolution fusion | flops 2415919104 | bytes 15728640 | tf_op jit(solution)/shard_map/sd,dcn->csn/dot_general | solution.py:150
  20.3 3.4 fusion.193
  34.6 2.6 convolution_convert_fusion.1
  37.3 11.7 %all-to-all-start = ((bf16[64,24,1024]{2,1,0:T(8,128)(2,1)}), bf16[64,24,1024]{2,1,0:T(8,128)(2,1)}, u32[]{:S(2)}, u32[]{:S(2)}) async-start(bf16[64,24,1024]{2,1,0:T(8,128)(2,1)} %bitcast.474), calls=%async_computation | async-start | bytes 6291456 | tf_op jit(solution)/shard_map/all_to_all | solution.py:97
  49.0 3.6 convolution_convert_fusion
  52.7 37.1 %all-to-all-done = bf16[64,24,1024]{2,1,0:T(8,128)(2,1)} async-done(((bf16[64,24,1024]{2,1,0:T(8,128)(2,1)}), bf16[64,24,1024]{2,1,0:T(8,128)(2,1)}, u32[]{:S(2)}, u32[]{:S(2)}) %all-to-all-start) | async-done | bytes 3145760 | tf_op jit(solution)/shard_map/all_to_all | solution.py:97
  89.8 8.0 %all-to-all-start.2 = ((bf16[64,24,1024]{2,1,0:T(8,128)(2,1)}), bf16[64,24,1024]{2,1,0:T(8,128)(2,1)}, u32[]{:S(2)}, u32[]{:S(2)}) async-start(bf16[64,24,1024]{2,1,0:T(8,128)(2,1)} %bitcast.473), calls=%async_computation.2 | async-start | bytes 6291456 | tf_op jit(solution)/shard_map/all_to_all | solution.py:97
  97.9 39.6 %all-to-all-done.2 = bf16[64,24,1024]{2,1,0:T(8,128)(2,1)} async-done(((bf16[64,24,1024]{2,1,0:T(8,128)(2,1)}), bf16[64,24,1024]{2,1,0:T(8,128)(2,1)}, u32[]{:S(2)}, u32[]{:S(2)}) %all-to-all-start.2) | async-done | bytes 3145760 | tf_op jit(solution)/shard_map/all_to_all | solution.py:97
  137.7 13.9 %fusion.13 = f32[1536,2,512]{0,2,1:T(8,128)} fusion(bf16[1536,1024]{1,0:T(8,128)(2,1)} %collective-permute-done.1, bf16[1536,1024]{1,0:T(8,128)(2,1)} %bitcast.9, pred[]{:T(512)S(6)} %eq.113, bf16[2048,2,512]{2,1,0:T(2,128)(2,1)} %bitcast.535), kind=kOutput, calls=%fused_computation.22 | convolution fusion | flops 6470762496 | bytes 16777216 | tf_op jit(solution)/shard_map/rd,dcf->rcf/dot_general | solution.py:196
  151.6 11.6 %fusion.23 = (f32[1536,1,512]{0,2,1:T(8,128)S(1)}, f32[1536]{0:T(1024)S(1)}, f32[1536,1,512]{0,2,1:T(8,128)}) fusion(f32[1536,2,512]{0,2,1:T(8,128)} %fusion.13, bf16[1,512,2048]{2,1,0:T(8,128)(2,1)S(1)} %copy-done, bf16[1536,1024]{1,0:T(8,128)(2,1)} %collective-permute-done.4, bf16[1536,1024]{1,0:T(8,128)(2,1)} %bitcast.17, pred[]{:T(512)S(6)} %eq.113), kind=kOutput, calls=%fused_computation.37 | convolution fusion | flops 3262118400 | bytes 20977664 | tf_op jit(solution)/shard_map/dot_general | solution.py:17
  163.2 9.9 %convolution_bitcast_fusion = f32[1536,2048]{1,0:T(8,128)S(1)} fusion(bf16[2048,2,512]{2,1,0:T(2,128)(2,1)S(1)} %bitcast.536, f32[1536,1,512]{0,2,1:T(8,128)} %get-tuple-element.97, f32[1536,1,512]{0,2,1:T(8,128)S(1)} %get-tuple-element.95), kind=kOutput, calls=%fused_computation.1 | convolution fusion | flops 6444023808 | bytes 23068672 | tf_op jit(solution)/shard_map/rcf,dcf->rd/dot_general | solution.py:219
  173.1 4.6 copy-done.21
  181.8 7.4 %all-to-all-start.4 = ((f32[64,8,128]{2,1,0:T(8,128)}), f32[64,8,128]{2,1,0:T(8,128)S(1)}, u32[]{:S(2)}, u32[]{:S(2)}) async-start(f32[64,8,128]{2,1,0:T(8,128)} %broadcast_in_dim.45), calls=%async_computation.4 | async-start | bytes 524288 | tf_op jit(solution)/shard_map/all_to_all | solution.py:97
  189.2 5.7 fusion.40
  194.9 4.6 copy-done.20
  203.4 10.3 %all-to-all-start.6 = ((f32[64,8,128]{2,1,0:T(8,128)}), f32[64,8,128]{2,1,0:T(8,128)S(1)}, u32[]{:S(2)}, u32[]{:S(2)}) async-start(f32[64,8,128]{2,1,0:T(8,128)} %broadcast_in_dim.49), calls=%async_computation.6 | async-start | bytes 524288 | tf_op jit(solution)/shard_map/all_to_all | solution.py:97
  213.7 6.6 %add_convert_fusion = bf16[1536,1024]{1,0:T(8,128)(2,1)} fusion(bf16[1536,1024]{1,0:T(8,128)(2,1)} %collective-permute-done.5, f32[1536,2048]{1,0:T(8,128)} %copy-done.21, s32[]{:T(128)S(6)} %select_n.392), kind=kLoop, calls=%fused_computation.7 | loop fusion | flops 4718592 | bytes 12582916 | tf_op jit(solution)/shard_map/convert_element_type | solution.py:215
  220.3 4.6 all-to-all-done.6
  224.9 6.1 all-to-all-start.3
  240.1 6.6 %add_convert_fusion.1 = bf16[1536,1024]{1,0:T(8,128)(2,1)} fusion(bf16[1536,1024]{1,0:T(8,128)(2,1)} %collective-permute-done.2, f32[1536,2048]{1,0:T(8,128)} %copy-done.20, s32[]{:T(128)S(6)} %select_n.392), kind=kLoop, calls=%fused_computation.9 | loop fusion | flops 4718592 | bytes 12582916 | tf_op jit(solution)/shard_map/convert_element_type | solution.py:215
  246.7 24.9 %all-to-all-done.3 = bf16[64,24,1024]{2,1,0:T(8,128)(2,1)} async-done(((bf16[64,24,1024]{2,1,0:T(8,128)(2,1)}), bf16[64,24,1024]{2,1,0:T(8,128)(2,1)}, u32[]{:S(2)}, u32[]{:S(2)}) %all-to-all-start.3) | async-done | bytes 3145760 | tf_op jit(solution)/shard_map/all_to_all | solution.py:97
  271.5 8.8 %all-to-all-start.1 = ((bf16[64,24,1024]{2,1,0:T(8,128)(2,1)}), bf16[64,24,1024]{2,1,0:T(8,128)(2,1)}, u32[]{:S(2)}, u32[]{:S(2)}) async-start(bf16[64,24,1024]{2,1,0:T(8,128)(2,1)} %bitcast.14), calls=%async_computation.1 | async-start | bytes 6291456 | tf_op jit(solution)/shard_map/all_to_all | solution.py:97
  282.3 16.7 %convolution_bitcast_fusion.1 = f32[1,2048,2,512]{3,1,2,0:T(8,128)} fusion(bf16[1536,1024]{1,0:T(8,128)(2,1)} %collective-permute-done.1, bf16[1536,1024]{1,0:T(8,128)(2,1)} %bitcast.9, pred[]{:T(512)S(6)} %eq.113, f32[1536,1,512]{0,2,1:T(8,128)} %get-tuple-element.97, f32[1536,1,512]{0,2,1:T(8,128)} %copy-done.96, f32[1536]{0:T(1024)S(1)} %mul.709), kind=kOutput, calls=%fused_computation.12 | convolution fusion | flops 6475481088 | bytes 20977664 | tf_op jit(solution)/shard_map/rd,rcf->dcf/dot_general | solution.py:224
  299.0 2.9 convolution_bitcast_fusion.4
  301.9 17.7 %all-to-all-done.1 = bf16[64,24,1024]{2,1,0:T(8,128)(2,1)} async-done(((bf16[64,24,1024]{2,1,0:T(8,128)(2,1)}), bf16[64,24,1024]{2,1,0:T(8,128)(2,1)}, u32[]{:S(2)}, u32[]{:S(2)}) %all-to-all-start.1) | async-done | bytes 3145760 | tf_op jit(solution)/shard_map/all_to_all | solution.py:97
  319.7 2.9 add_convert_fusion.5
  322.7 12.4 %convolution_bitcast_fusion.2 = f32[1,512,2048]{2,1,0:T(8,128)} fusion(f32[1536]{0:T(1024)S(1)} %mul.709, f32[1536,2,512]{0,2,1:T(8,128)} %fusion.13, bf16[1536,1024]{1,0:T(8,128)(2,1)} %collective-permute-done.4, bf16[1536,1024]{1,0:T(8,128)(2,1)} %bitcast.17, pred[]{:T(512)S(6)} %eq.113), kind=kOutput, calls=%fused_computation.28 | convolution fusion | flops 3255042048 | bytes 16783360 | tf_op jit(solution)/shard_map/dot_general | solution.py:17
  335.2 17.0 %copy.264 = f32[1,2048,2,512]{3,2,1,0:T(2,128)} copy(f32[1,2048,2,512]{3,1,2,0:T(8,128)S(1)} %bitcast.487) | data formatting | bytes 16777216
  353.3 2.8 multiply_reduce_fusion.1
  357.1 3.3 convolution_convert_fusion.2
  377.1 2.7 fusion.58
  381.0 7.0 %all-to-all-start.5 = ((f32[64,17,128]{2,1,0:T(8,128)}), f32[64,17,128]{2,1,0:T(8,128)}, u32[]{:S(2)}, u32[]{:S(2)}) async-start(f32[64,17,128]{2,1,0:T(8,128)} %reshape.490), calls=%async_computation.5 | async-start | bytes 1572864 | tf_op jit(solution)/shard_map/all_to_all | solution.py:97
  388.0 4.1 fusion.192
  398.8 3.7 fusion.5
  403.0 3.8 fusion.3
  407.3 4.7 fusion.32
  415.8 3.0 collective-permute-start.48
  425.4 2.8 collective-permute-start.51
  434.0 3.0 collective-permute-start.75
  437.8 2.7 collective-permute-start.54
  449.2 2.7 collective-permute-start.78
  454.1 3.5 collective-permute-done.79
  473.2 3.2 collective-permute-done.12
  478.8 3.8 collective-permute-done.22
  487.4 9.8 %collective-permute-done.33 = bf16[192,512]{0,1:T(8,128)(2,1)S(1)} collective-permute-done((bf16[192,512]{0,1:T(8,128)(2,1)S(1)}, bf16[192,512]{0,1:T(8,128)(2,1)S(1)}, u32[]{:S(2)}, u32[]{:S(2)}) %collective-permute-start.33) | collective-permute-done | bytes 196640 | tf_op jit(solution)/shard_map/ppermute | solution.py:64
  499.9 3.7 collective-permute-done.35
  505.2 2.8 collective-permute-start.57
  508.5 9.0 %collective-permute-done.56 = bf16[4,4,32,384]{3,2,0,1:T(8,128)(2,1)S(1)} collective-permute-done((bf16[4,4,32,384]{3,2,0,1:T(8,128)(2,1)S(1)}, bf16[4,4,32,384]{3,2,0,1:T(8,128)(2,1)S(1)}, u32[]{:S(2)}, u32[]{:S(2)}) %collective-permute-start.56) | collective-permute-done | bytes 393248 | tf_op jit(solution)/shard_map/ppermute | solution.py:64
  517.5 4.3 collective-permute-done.57
  521.8 2.8 collective-permute-start.38
  525.1 3.3 collective-permute-start.66
  530.1 5.2 collective-permute-done.65
  548.0 2.6 collective-permute-start.69
  554.2 3.7 collective-permute-start.63
  559.4 3.7 collective-permute-start.72
  566.9 2.9 collective-permute-start.17
  573.1 2.6 collective-permute-start.28
  577.8 2.8 collective-permute-start.40
  580.5 3.5 collective-permute-done.28
  586.5 2.8 collective-permute-start.19
  589.3 3.0 collective-permute-start.20
  593.8 2.6 collective-permute-start.31
  603.4 3.6 collective-permute-done.44
  612.8 3.1 fusion.48
  (514 shorter events, 171.1 us)
Async XLA Ops:
  37.3 52.5 %all-to-all-start = ((bf16[64,24,1024]{2,1,0:T(8,128)(2,1)}), bf16[64,24,1024]{2,1,0:T(8,128)(2,1)}, u32[]{:S(2)}, u32[]{:S(2)}) async-start(bf16[64,24,1024]{2,1,0:T(8,128)(2,1)} %bitcast.474), calls=%async_computation | async-start | bytes 6291456 | tf_op jit(solution)/shard_map/all_to_all | solution.py:97
  89.8 47.7 %all-to-all-start.2 = ((bf16[64,24,1024]{2,1,0:T(8,128)(2,1)}), bf16[64,24,1024]{2,1,0:T(8,128)(2,1)}, u32[]{:S(2)}, u32[]{:S(2)}) async-start(bf16[64,24,1024]{2,1,0:T(8,128)(2,1)} %bitcast.473), calls=%async_computation.2 | async-start | bytes 6291456 | tf_op jit(solution)/shard_map/all_to_all | solution.py:97
  97.8 39.9 %collective-permute-start.1 = (bf16[1536,1024]{1,0:T(8,128)(2,1)}, bf16[1536,1024]{1,0:T(8,128)(2,1)}, u32[]{:S(2)}, u32[]{:S(2)}) collective-permute-start(bf16[1536,1024]{1,0:T(8,128)(2,1)} %bitcast.9), channel_id=1, source_target_pairs={{0,1},{1,0},{2,3},{3,2},{4,5},{5,4},{6,7},{7,6},{8,9},{9,8},{10,11... | collective-permute-start | bytes 9437192 | tf_op jit(solution)/shard_map/ppermute | solution.py:60
  137.5 14.1 %collective-permute-start.4 = (bf16[1536,1024]{1,0:T(8,128)(2,1)}, bf16[1536,1024]{1,0:T(8,128)(2,1)}, u32[]{:S(2)}, u32[]{:S(2)}) collective-permute-start(bf16[1536,1024]{1,0:T(8,128)(2,1)} %bitcast.17), channel_id=1, source_target_pairs={{0,1},{1,0},{2,3},{3,2},{4,5},{5,4},{6,7},{7,6},{8,9},{9,8},{10,11... | collective-permute-start | bytes 9437192 | tf_op jit(solution)/shard_map/ppermute | solution.py:60
  179.9 33.8 %collective-permute-start.5 = (bf16[1536,1024]{1,0:T(8,128)(2,1)}, bf16[1536,1024]{1,0:T(8,128)(2,1)}, u32[]{:S(2)}, u32[]{:S(2)}) collective-permute-start(bf16[1536,1024]{1,0:T(8,128)(2,1)} %dynamic-slice_convert_fusion), channel_id=1, source_target_pairs={{0,1},{1,0},{2,3},{3,2},{4,5},{5,4},{6,7},{7,6},{8,9},{9,8},{10,11... | collective-permute-start | bytes 9437192 | tf_op jit(solution)/shard_map/ppermute | solution.py:60
  181.8 20.0 %all-to-all-start.4 = ((f32[64,8,128]{2,1,0:T(8,128)}), f32[64,8,128]{2,1,0:T(8,128)S(1)}, u32[]{:S(2)}, u32[]{:S(2)}) async-start(f32[64,8,128]{2,1,0:T(8,128)} %broadcast_in_dim.45), calls=%async_computation.4 | async-start | bytes 524288 | tf_op jit(solution)/shard_map/all_to_all | solution.py:97
  201.6 38.4 %collective-permute-start.2 = (bf16[1536,1024]{1,0:T(8,128)(2,1)}, bf16[1536,1024]{1,0:T(8,128)(2,1)}, u32[]{:S(2)}, u32[]{:S(2)}) collective-permute-start(bf16[1536,1024]{1,0:T(8,128)(2,1)} %dynamic-slice_convert_fusion.1), channel_id=1, source_target_pairs={{0,1},{1,0},{2,3},{3,2},{4,5},{5,4},{6,7},{7,6},{8,9},{9,8},{10,11... | collective-permute-start | bytes 9437192 | tf_op jit(solution)/shard_map/ppermute | solution.py:60
  203.4 21.5 %all-to-all-start.6 = ((f32[64,8,128]{2,1,0:T(8,128)}), f32[64,8,128]{2,1,0:T(8,128)S(1)}, u32[]{:S(2)}, u32[]{:S(2)}) async-start(f32[64,8,128]{2,1,0:T(8,128)} %broadcast_in_dim.49), calls=%async_computation.6 | async-start | bytes 524288 | tf_op jit(solution)/shard_map/all_to_all | solution.py:97
  224.9 46.6 %all-to-all-start.3 = ((bf16[64,24,1024]{2,1,0:T(8,128)(2,1)}), bf16[64,24,1024]{2,1,0:T(8,128)(2,1)}, u32[]{:S(2)}, u32[]{:S(2)}) async-start(bf16[64,24,1024]{2,1,0:T(8,128)(2,1)} %bitcast.23), calls=%async_computation.3 | async-start | bytes 6291456 | tf_op jit(solution)/shard_map/all_to_all | solution.py:97
  232.7 235.4 %collective-permute-start.9 = (bf16[192,512]{0,1:T(8,128)(2,1)}, bf16[192,512]{0,1:T(8,128)(2,1)}, u32[]{:S(2)}, u32[]{:S(2)}) collective-permute-start(bf16[192,512]{0,1:T(8,128)(2,1)} %bitcast.35), channel_id=1, source_target_pairs={{0,32},{32,64},{64,96},{96,0},{1,33},{33,65},{65,97},{97,1},{2,34}... | collective-permute-start | bytes 589832 | tf_op jit(solution)/shard_map/ppermute | solution.py:64
  271.5 48.1 %all-to-all-start.1 = ((bf16[64,24,1024]{2,1,0:T(8,128)(2,1)}), bf16[64,24,1024]{2,1,0:T(8,128)(2,1)}, u32[]{:S(2)}, u32[]{:S(2)}) async-start(bf16[64,24,1024]{2,1,0:T(8,128)(2,1)} %bitcast.14), calls=%async_computation.1 | async-start | bytes 6291456 | tf_op jit(solution)/shard_map/all_to_all | solution.py:97
  301.9 51.4 %collective-permute-start.6 = (f32[192,1024]{1,0:T(8,128)S(1)}, f32[192,1024]{1,0:T(8,128)}, u32[]{:S(2)}, u32[]{:S(2)}) collective-permute-start(f32[192,1024]{1,0:T(8,128)S(1)} %convolution_bitcast_fusion.4), channel_id=1, source_target_pairs={{0,1},{1,0},{2,3},{3,2},{4,5},{5,4},{6,7},{7,6},{8,9},{9,8},{10,11... | collective-permute-start | bytes 2359304 | tf_op jit(solution)/shard_map/ppermute | solution.py:60
  322.6 29.5 %collective-permute-start.3 = (bf16[192,1024]{1,0:T(8,128)(2,1)S(1)}, bf16[192,1024]{1,0:T(8,128)(2,1)S(1)}, u32[]{:S(2)}, u32[]{:S(2)}) collective-permute-start(bf16[192,1024]{1,0:T(8,128)(2,1)S(1)} %add_convert_fusion.5), channel_id=1, source_target_pairs={{0,1},{1,0},{2,3},{3,2},{4,5},{5,4},{6,7},{7,6},{8,9},{9,8},{10,11... | collective-permute-start | bytes 1179656 | tf_op jit(solution)/shard_map/ppermute | solution.py:60
  381.0 190.2 %all-to-all-start.5 = ((f32[64,17,128]{2,1,0:T(8,128)}), f32[64,17,128]{2,1,0:T(8,128)}, u32[]{:S(2)}, u32[]{:S(2)}) async-start(f32[64,17,128]{2,1,0:T(8,128)} %reshape.490), calls=%async_computation.5 | async-start | bytes 1572864 | tf_op jit(solution)/shard_map/all_to_all | solution.py:97
  398.7 15.5 %collective-permute-start.46 = (f32[2,128]{1,0:T(2,128)S(1)}, f32[2,128]{1,0:T(2,128)S(1)}, u32[]{:S(2)}, u32[]{:S(2)}) collective-permute-start(f32[2,128]{1,0:T(2,128)S(1)} %pad_maximum_fusion.7), channel_id=1, source_target_pairs={{0,1},{1,0},{2,3},{3,2},{4,5},{5,4},{6,7},{7,6},{8,9},{9,8},{10,11... | collective-permute-start | bytes 3080 | tf_op jit(solution)/shard_map/ppermute | solution.py:60
  422.4 7.3 %collective-permute-start.50 = (f32[2,128]{1,0:T(2,128)S(1)}, f32[2,128]{1,0:T(2,128)S(1)}, u32[]{:S(2)}, u32[]{:S(2)}) collective-permute-start(f32[2,128]{1,0:T(2,128)S(1)} %bitcast.532), channel_id=1, source_target_pairs={{0,8},{8,16},{16,24},{24,0},{1,9},{9,17},{17,25},{25,1},{2,10},{10... | collective-permute-start | bytes 3080 | tf_op jit(solution)/shard_map/ppermute | solution.py:64
  433.7 14.6 %collective-permute-start.74 = (bf16[4,4,32,256]{3,2,1,0:T(8,128)(2,1)S(1)}, bf16[4,4,32,256]{3,2,1,0:T(8,128)(2,1)S(1)}, u32[]{:S(2)}, u32[]{:S(2)}) collective-permute-start(bf16[4,4,32,256]{3,2,1,0:T(8,128)(2,1)S(1)} %get-tuple-element.111), channel_id=1, source_target_pairs={{0,32},{32,64},{64,96},{96,0},{1,33},{33,65},{65,97},{97,1},{2,34}... | collective-permute-start | bytes 786440 | tf_op jit(solution)/shard_map/ppermute | solution.py:64
  434.0 14.3 %collective-permute-start.75 = (bf16[4,4,32,256]{3,2,1,0:T(8,128)(2,1)S(1)}, bf16[4,4,32,256]{3,2,1,0:T(8,128)(2,1)S(1)}, u32[]{:S(2)}, u32[]{:S(2)}) collective-permute-start(bf16[4,4,32,256]{3,2,1,0:T(8,128)(2,1)S(1)} %get-tuple-element.113), channel_id=1, source_target_pairs={{0,96},{32,0},{64,32},{96,64},{1,97},{33,1},{65,33},{97,65},{2,98}... | collective-permute-start | bytes 786440 | tf_op jit(solution)/shard_map/ppermute | solution.py:64
  437.0 11.3 %collective-permute-start.76 = (bf16[4,4,32,256]{3,2,1,0:T(8,128)(2,1)S(1)}, bf16[4,4,32,256]{3,2,1,0:T(8,128)(2,1)S(1)}, u32[]{:S(2)}, u32[]{:S(2)}) collective-permute-start(bf16[4,4,32,256]{3,2,1,0:T(8,128)(2,1)S(1)} %get-tuple-element.112), channel_id=1, source_target_pairs={{0,64},{32,96},{64,0},{96,32},{1,65},{33,97},{65,1},{97,33},{2,66}... | collective-permute-start | bytes 786440 | tf_op jit(solution)/shard_map/ppermute | solution.py:64
  446.8 21.3 %collective-permute-start.10 = (bf16[192,1024]{1,0:T(8,128)(2,1)S(1)}, bf16[192,1024]{1,0:T(8,128)(2,1)S(1)}, u32[]{:S(2)}, u32[]{:S(2)}) collective-permute-start(bf16[192,1024]{1,0:T(8,128)(2,1)S(1)} %get-tuple-element.100), channel_id=1, source_target_pairs={{0,32},{32,64},{64,96},{96,0},{1,33},{33,65},{65,97},{97,1},{2,34}... | collective-permute-start | bytes 1179656 | tf_op jit(solution)/shard_map/ppermute | solution.py:64
  463.0 8.8 %collective-permute-start.11 = (bf16[192,512]{0,1:T(8,128)(2,1)S(1)}, bf16[192,512]{0,1:T(8,128)(2,1)S(1)}, u32[]{:S(2)}, u32[]{:S(2)}) collective-permute-start(bf16[192,512]{0,1:T(8,128)(2,1)S(1)} %bitcast.516), channel_id=1, source_target_pairs={{0,96},{32,0},{64,32},{96,64},{1,97},{33,1},{65,33},{97,65},{2,98}... | collective-permute-start | bytes 589832 | tf_op jit(solution)/shard_map/ppermute | solution.py:64
  464.9 40.4 %collective-permute-start.13 = (bf16[192,512]{0,1:T(8,128)(2,1)S(1)}, bf16[192,512]{0,1:T(8,128)(2,1)S(1)}, u32[]{:S(2)}, u32[]{:S(2)}) collective-permute-start(bf16[192,512]{0,1:T(8,128)(2,1)S(1)} %bitcast.515), channel_id=1, source_target_pairs={{0,64},{32,96},{64,0},{96,32},{1,65},{33,97},{65,1},{97,33},{2,66}... | collective-permute-start | bytes 589832 | tf_op jit(solution)/shard_map/ppermute | solution.py:64
  466.4 10.1 %collective-permute-start.12 = (bf16[192,1024]{1,0:T(8,128)(2,1)S(1)}, bf16[192,1024]{1,0:T(8,128)(2,1)S(1)}, u32[]{:S(2)}, u32[]{:S(2)}) collective-permute-start(bf16[192,1024]{1,0:T(8,128)(2,1)S(1)} %get-tuple-element.100), channel_id=1, source_target_pairs={{0,96},{32,0},{64,32},{96,64},{1,97},{33,1},{65,33},{97,65},{2,98}... | collective-permute-start | bytes 1179656 | tf_op jit(solution)/shard_map/ppermute | solution.py:64
  468.1 10.4 %collective-permute-start.21 = (bf16[192,512]{0,1:T(8,128)(2,1)S(1)}, bf16[192,512]{0,1:T(8,128)(2,1)S(1)}, u32[]{:S(2)}, u32[]{:S(2)}) collective-permute-start(bf16[192,512]{0,1:T(8,128)(2,1)S(1)} %bitcast.522), channel_id=1, source_target_pairs={{0,8},{8,16},{16,24},{24,0},{1,9},{9,17},{17,25},{25,1},{2,10},{10... | collective-permute-start | bytes 589832 | tf_op jit(solution)/shard_map/ppermute | solution.py:64
  468.2 14.4 %collective-permute-start.22 = (bf16[192,1024]{1,0:T(8,128)(2,1)S(1)}, bf16[192,1024]{1,0:T(8,128)(2,1)S(1)}, u32[]{:S(2)}, u32[]{:S(2)}) collective-permute-start(bf16[192,1024]{1,0:T(8,128)(2,1)S(1)} %get-tuple-element.101), channel_id=1, source_target_pairs={{0,8},{8,16},{16,24},{24,0},{1,9},{9,17},{17,25},{25,1},{2,10},{10... | collective-permute-start | bytes 1179656 | tf_op jit(solution)/shard_map/ppermute | solution.py:64
  471.8 11.8 %collective-permute-start.23 = (bf16[192,512]{0,1:T(8,128)(2,1)S(1)}, bf16[192,512]{0,1:T(8,128)(2,1)S(1)}, u32[]{:S(2)}, u32[]{:S(2)}) collective-permute-start(bf16[192,512]{0,1:T(8,128)(2,1)S(1)} %bitcast.521), channel_id=1, source_target_pairs={{0,24},{8,0},{16,8},{24,16},{1,25},{9,1},{17,9},{25,17},{2,26},{10... | collective-permute-start | bytes 589832 | tf_op jit(solution)/shard_map/ppermute | solution.py:64
  476.5 8.6 %collective-permute-start.24 = (bf16[192,1024]{1,0:T(8,128)(2,1)S(1)}, bf16[192,1024]{1,0:T(8,128)(2,1)S(1)}, u32[]{:S(2)}, u32[]{:S(2)}) collective-permute-start(bf16[192,1024]{1,0:T(8,128)(2,1)S(1)} %get-tuple-element.101), channel_id=1, source_target_pairs={{0,24},{8,0},{16,8},{24,16},{1,25},{9,1},{17,9},{25,17},{2,26},{10... | collective-permute-start | bytes 1179656 | tf_op jit(solution)/shard_map/ppermute | solution.py:64
  478.5 46.6 %collective-permute-start.25 = (bf16[192,512]{0,1:T(8,128)(2,1)S(1)}, bf16[192,512]{0,1:T(8,128)(2,1)S(1)}, u32[]{:S(2)}, u32[]{:S(2)}) collective-permute-start(bf16[192,512]{0,1:T(8,128)(2,1)S(1)} %bitcast.518), channel_id=1, source_target_pairs={{0,16},{8,24},{16,0},{24,8},{1,17},{9,25},{17,1},{25,9},{2,18},{10... | collective-permute-start | bytes 589832 | tf_op jit(solution)/shard_map/ppermute | solution.py:64
  482.6 14.9 %collective-permute-start.34 = (bf16[192,1024]{1,0:T(8,128)(2,1)S(1)}, bf16[192,1024]{1,0:T(8,128)(2,1)S(1)}, u32[]{:S(2)}, u32[]{:S(2)}) collective-permute-start(bf16[192,1024]{1,0:T(8,128)(2,1)S(1)} %bitcast.509), channel_id=1, source_target_pairs={{0,2},{2,4},{4,6},{6,0},{1,3},{3,5},{5,7},{7,1},{8,10},{10,12},{12... | collective-permute-start | bytes 1179656 | tf_op jit(solution)/shard_map/ppermute | solution.py:64
  483.7 13.5 %collective-permute-start.33 = (bf16[192,512]{0,1:T(8,128)(2,1)S(1)}, bf16[192,512]{0,1:T(8,128)(2,1)S(1)}, u32[]{:S(2)}, u32[]{:S(2)}) collective-permute-start(bf16[192,512]{0,1:T(8,128)(2,1)S(1)} %bitcast.520), channel_id=1, source_target_pairs={{0,2},{2,4},{4,6},{6,0},{1,3},{3,5},{5,7},{7,1},{8,10},{10,12},{12... | collective-permute-start | bytes 589832 | tf_op jit(solution)/shard_map/ppermute | solution.py:64
  485.0 19.3 %collective-permute-start.36 = (bf16[192,1024]{1,0:T(8,128)(2,1)S(1)}, bf16[192,1024]{1,0:T(8,128)(2,1)S(1)}, u32[]{:S(2)}, u32[]{:S(2)}) collective-permute-start(bf16[192,1024]{1,0:T(8,128)(2,1)S(1)} %bitcast.510), channel_id=1, source_target_pairs={{0,6},{2,0},{4,2},{6,4},{1,7},{3,1},{5,3},{7,5},{8,14},{10,8},{12,... | collective-permute-start | bytes 1179656 | tf_op jit(solution)/shard_map/ppermute | solution.py:64
  497.2 6.4 %collective-permute-start.35 = (bf16[192,512]{0,1:T(8,128)(2,1)S(1)}, bf16[192,512]{0,1:T(8,128)(2,1)S(1)}, u32[]{:S(2)}, u32[]{:S(2)}) collective-permute-start(bf16[192,512]{0,1:T(8,128)(2,1)S(1)} %bitcast.519), channel_id=1, source_target_pairs={{0,6},{2,0},{4,2},{6,4},{1,7},{3,1},{5,3},{7,5},{8,14},{10,8},{12,... | collective-permute-start | bytes 589832 | tf_op jit(solution)/shard_map/ppermute | solution.py:64
  497.5 10.6 %collective-permute-start.14 = (bf16[192,1024]{1,0:T(8,128)(2,1)S(1)}, bf16[192,1024]{1,0:T(8,128)(2,1)S(1)}, u32[]{:S(2)}, u32[]{:S(2)}) collective-permute-start(bf16[192,1024]{1,0:T(8,128)(2,1)S(1)} %get-tuple-element.100), channel_id=1, source_target_pairs={{0,64},{32,96},{64,0},{96,32},{1,65},{33,97},{65,1},{97,33},{2,66}... | collective-permute-start | bytes 1179656 | tf_op jit(solution)/shard_map/ppermute | solution.py:64
  503.6 40.1 %collective-permute-start.37 = (bf16[192,512]{0,1:T(8,128)(2,1)S(1)}, bf16[192,512]{0,1:T(8,128)(2,1)S(1)}, u32[]{:S(2)}, u32[]{:S(2)}) collective-permute-start(bf16[192,512]{0,1:T(8,128)(2,1)S(1)} %bitcast.517), channel_id=1, source_target_pairs={{0,4},{2,6},{4,0},{6,2},{1,5},{3,7},{5,1},{7,3},{8,12},{10,14},{12... | collective-permute-start | bytes 589832 | tf_op jit(solution)/shard_map/ppermute | solution.py:64
  504.3 13.2 %collective-permute-start.56 = (bf16[4,4,32,384]{3,2,0,1:T(8,128)(2,1)S(1)}, bf16[4,4,32,384]{3,2,0,1:T(8,128)(2,1)S(1)}, u32[]{:S(2)}, u32[]{:S(2)}) collective-permute-start(bf16[4,4,32,384]{3,2,0,1:T(8,128)(2,1)S(1)} %bitcast.514), channel_id=1, source_target_pairs={{0,8},{8,16},{16,24},{24,0},{1,9},{9,17},{17,25},{25,1},{2,10},{10... | collective-permute-start | bytes 1179656 | tf_op jit(solution)/shard_map/ppermute | solution.py:64
  505.2 16.6 %collective-permute-start.57 = (bf16[4,4,32,384]{3,2,0,1:T(8,128)(2,1)S(1)}, bf16[4,4,32,384]{3,2,0,1:T(8,128)(2,1)S(1)}, u32[]{:S(2)}, u32[]{:S(2)}) collective-permute-start(bf16[4,4,32,384]{3,2,0,1:T(8,128)(2,1)S(1)} %bitcast.513), channel_id=1, source_target_pairs={{0,24},{8,0},{16,8},{24,16},{1,25},{9,1},{17,9},{25,17},{2,26},{10... | collective-permute-start | bytes 1179656 | tf_op jit(solution)/shard_map/ppermute | solution.py:64
  508.1 16.5 %collective-permute-start.58 = (bf16[4,4,32,384]{3,2,0,1:T(8,128)(2,1)S(1)}, bf16[4,4,32,384]{3,2,0,1:T(8,128)(2,1)S(1)}, u32[]{:S(2)}, u32[]{:S(2)}) collective-permute-start(bf16[4,4,32,384]{3,2,0,1:T(8,128)(2,1)S(1)} %bitcast.512), channel_id=1, source_target_pairs={{0,16},{8,24},{16,0},{24,8},{1,17},{9,25},{17,1},{25,9},{2,18},{10... | collective-permute-start | bytes 1179656 | tf_op jit(solution)/shard_map/ppermute | solution.py:64
  517.5 10.8 %collective-permute-start.26 = (bf16[192,1024]{1,0:T(8,128)(2,1)S(1)}, bf16[192,1024]{1,0:T(8,128)(2,1)S(1)}, u32[]{:S(2)}, u32[]{:S(2)}) collective-permute-start(bf16[192,1024]{1,0:T(8,128)(2,1)S(1)} %get-tuple-element.101), channel_id=1, source_target_pairs={{0,16},{8,24},{16,0},{24,8},{1,17},{9,25},{17,1},{25,9},{2,18},{10... | collective-permute-start | bytes 1179656 | tf_op jit(solution)/shard_map/ppermute | solution.py:64
  521.8 24.1 %collective-permute-start.38 = (bf16[192,1024]{1,0:T(8,128)(2,1)S(1)}, bf16[192,1024]{1,0:T(8,128)(2,1)S(1)}, u32[]{:S(2)}, u32[]{:S(2)}) collective-permute-start(bf16[192,1024]{1,0:T(8,128)(2,1)S(1)} %bitcast.511), channel_id=1, source_target_pairs={{0,4},{2,6},{4,0},{6,2},{1,5},{3,7},{5,1},{7,3},{8,12},{10,14},{12... | collective-permute-start | bytes 1179656 | tf_op jit(solution)/shard_map/ppermute | solution.py:64
  524.6 10.7 %collective-permute-start.65 = (bf16[4,4,32,384]{3,2,1,0:T(8,128)(2,1)S(1)}, bf16[4,4,32,384]{3,2,1,0:T(8,128)(2,1)S(1)}, u32[]{:S(2)}, u32[]{:S(2)}) collective-permute-start(bf16[4,4,32,384]{3,2,1,0:T(8,128)(2,1)S(1)} %get-tuple-element.108), channel_id=1, source_target_pairs={{0,2},{2,4},{4,6},{6,0},{1,3},{3,5},{5,7},{7,1},{8,10},{10,12},{12... | collective-permute-start | bytes 1179656 | tf_op jit(solution)/shard_map/ppermute | solution.py:64
  525.1 12.8 %collective-permute-start.66 = (bf16[4,4,32,384]{3,2,1,0:T(8,128)(2,1)S(1)}, bf16[4,4,32,384]{3,2,1,0:T(8,128)(2,1)S(1)}, u32[]{:S(2)}, u32[]{:S(2)}) collective-permute-start(bf16[4,4,32,384]{3,2,1,0:T(8,128)(2,1)S(1)} %get-tuple-element.110), channel_id=1, source_target_pairs={{0,6},{2,0},{4,2},{6,4},{1,7},{3,1},{5,3},{7,5},{8,14},{10,8},{12,... | collective-permute-start | bytes 1179656 | tf_op jit(solution)/shard_map/ppermute | solution.py:64
  528.3 11.8 %collective-permute-start.67 = (bf16[4,4,32,384]{3,2,1,0:T(8,128)(2,1)S(1)}, bf16[4,4,32,384]{3,2,1,0:T(8,128)(2,1)S(1)}, u32[]{:S(2)}, u32[]{:S(2)}) collective-permute-start(bf16[4,4,32,384]{3,2,1,0:T(8,128)(2,1)S(1)} %get-tuple-element.109), channel_id=1, source_target_pairs={{0,4},{2,6},{4,0},{6,2},{1,5},{3,7},{5,1},{7,3},{8,12},{10,14},{12... | collective-permute-start | bytes 1179656 | tf_op jit(solution)/shard_map/ppermute | solution.py:64
  535.3 75.4 %collective-permute-start.8 = (bf16[192,2048]{1,0:T(8,128)(2,1)}, bf16[192,2048]{1,0:T(8,128)(2,1)}, u32[]{:S(2)}, u32[]{:S(2)}) collective-permute-start(bf16[192,2048]{1,0:T(8,128)(2,1)} %fusion.32), channel_id=1, source_target_pairs={{0,1},{1,0},{2,3},{3,2},{4,5},{5,4},{6,7},{7,6},{8,9},{9,8},{10,11... | collective-permute-start | bytes 2359304 | tf_op jit(solution)/shard_map/ppermute | solution.py:60
  537.9 10.1 %collective-permute-start.59 = (bf16[4,32,384]{2,1,0:T(8,128)(2,1)S(1)}, bf16[4,32,384]{2,1,0:T(8,128)(2,1)S(1)}, u32[]{:S(2)}, u32[]{:S(2)}) collective-permute-start(bf16[4,32,384]{2,1,0:T(8,128)(2,1)S(1)} %get-tuple-element.143), channel_id=1, source_target_pairs={{0,2},{2,4},{4,6},{6,0},{1,3},{3,5},{5,7},{7,1},{8,10},{10,12},{12... | collective-permute-start | bytes 294920 | tf_op jit(solution)/shard_map/ppermute | solution.py:64
  540.2 10.4 %collective-permute-start.60 = (bf16[4,32,384]{2,1,0:T(8,128)(2,1)S(1)}, bf16[4,32,384]{2,1,0:T(8,128)(2,1)S(1)}, u32[]{:S(2)}, u32[]{:S(2)}) collective-permute-start(bf16[4,32,384]{2,1,0:T(8,128)(2,1)S(1)} %get-tuple-element.145), channel_id=1, source_target_pairs={{0,6},{2,0},{4,2},{6,4},{1,7},{3,1},{5,3},{7,5},{8,14},{10,8},{12,... | collective-permute-start | bytes 294920 | tf_op jit(solution)/shard_map/ppermute | solution.py:64
  543.7 8.0 %collective-permute-start.61 = (bf16[4,32,384]{2,1,0:T(8,128)(2,1)S(1)}, bf16[4,32,384]{2,1,0:T(8,128)(2,1)S(1)}, u32[]{:S(2)}, u32[]{:S(2)}) collective-permute-start(bf16[4,32,384]{2,1,0:T(8,128)(2,1)S(1)} %get-tuple-element.144), channel_id=1, source_target_pairs={{0,4},{2,6},{4,0},{6,2},{1,5},{3,7},{5,1},{7,3},{8,12},{10,14},{12... | collective-permute-start | bytes 294920 | tf_op jit(solution)/shard_map/ppermute | solution.py:64
  550.5 7.3 %collective-permute-start.70 = (bf16[4,32,384]{2,1,0:T(8,128)(2,1)S(1)}, bf16[4,32,384]{2,1,0:T(8,128)(2,1)S(1)}, u32[]{:S(2)}, u32[]{:S(2)}) collective-permute-start(bf16[4,32,384]{2,1,0:T(8,128)(2,1)S(1)} %get-tuple-element.147), channel_id=1, source_target_pairs={{0,64},{32,96},{64,0},{96,32},{1,65},{33,97},{65,1},{97,33},{2,66}... | collective-permute-start | bytes 294920 | tf_op jit(solution)/shard_map/ppermute | solution.py:64
  551.7 21.3 %collective-permute-start.15 = (bf16[4,32,1024]{2,1,0:T(8,128)(2,1)}, bf16[4,32,1024]{2,1,0:T(8,128)(2,1)}, u32[]{:S(2)}, u32[]{:S(2)}) collective-permute-start(bf16[4,32,1024]{2,1,0:T(8,128)(2,1)} %get-tuple-element.114), channel_id=1, source_target_pairs={{0,8},{8,16},{16,24},{24,0},{1,9},{9,17},{17,25},{25,1},{2,10},{10... | collective-permute-start | bytes 786440 | tf_op jit(solution)/shard_map/ppermute | solution.py:64
  558.0 7.7 %collective-permute-start.71 = (bf16[32,384]{1,0:T(8,128)(2,1)S(1)}, bf16[32,384]{1,0:T(8,128)(2,1)S(1)}, u32[]{:S(2)}, u32[]{:S(2)}) collective-permute-start(bf16[32,384]{1,0:T(8,128)(2,1)S(1)} %get-tuple-element.168), channel_id=1, source_target_pairs={{0,8},{8,16},{16,24},{24,0},{1,9},{9,17},{17,25},{25,1},{2,10},{10... | collective-permute-start | bytes 73736 | tf_op jit(solution)/shard_map/ppermute | solution.py:64
  559.4 7.6 %collective-permute-start.72 = (bf16[32,384]{1,0:T(8,128)(2,1)S(1)}, bf16[32,384]{1,0:T(8,128)(2,1)S(1)}, u32[]{:S(2)}, u32[]{:S(2)}) collective-permute-start(bf16[32,384]{1,0:T(8,128)(2,1)S(1)} %get-tuple-element.170), channel_id=1, source_target_pairs={{0,24},{8,0},{16,8},{24,16},{1,25},{9,1},{17,9},{25,17},{2,26},{10... | collective-permute-start | bytes 73736 | tf_op jit(solution)/shard_map/ppermute | solution.py:64
  563.2 6.7 %collective-permute-start.73 = (bf16[32,384]{1,0:T(8,128)(2,1)S(1)}, bf16[32,384]{1,0:T(8,128)(2,1)S(1)}, u32[]{:S(2)}, u32[]{:S(2)}) collective-permute-start(bf16[32,384]{1,0:T(8,128)(2,1)S(1)} %get-tuple-element.169), channel_id=1, source_target_pairs={{0,16},{8,24},{16,0},{24,8},{1,17},{9,25},{17,1},{25,9},{2,18},{10... | collective-permute-start | bytes 73736 | tf_op jit(solution)/shard_map/ppermute | solution.py:64
  565.7 10.0 %collective-permute-start.16 = (bf16[4,32,1024]{2,1,0:T(8,128)(2,1)}, bf16[4,32,1024]{2,1,0:T(8,128)(2,1)}, u32[]{:S(2)}, u32[]{:S(2)}) collective-permute-start(bf16[4,32,1024]{2,1,0:T(8,128)(2,1)} %get-tuple-element.116), channel_id=1, source_target_pairs={{0,24},{8,0},{16,8},{24,16},{1,25},{9,1},{17,9},{25,17},{2,26},{10... | collective-permute-start | bytes 786440 | tf_op jit(solution)/shard_map/ppermute | solution.py:64
  566.9 8.9 %collective-permute-start.17 = (bf16[4,32,1024]{2,1,0:T(8,128)(2,1)}, bf16[4,32,1024]{2,1,0:T(8,128)(2,1)}, u32[]{:S(2)}, u32[]{:S(2)}) collective-permute-start(bf16[4,32,1024]{2,1,0:T(8,128)(2,1)} %get-tuple-element.115), channel_id=1, source_target_pairs={{0,16},{8,24},{16,0},{24,8},{1,17},{9,25},{17,1},{25,9},{2,18},{10... | collective-permute-start | bytes 786440 | tf_op jit(solution)/shard_map/ppermute | solution.py:64
  569.9 7.9 %collective-permute-start.27 = (bf16[4,32,1024]{2,1,0:T(8,128)(2,1)}, bf16[4,32,1024]{2,1,0:T(8,128)(2,1)}, u32[]{:S(2)}, u32[]{:S(2)}) collective-permute-start(bf16[4,32,1024]{2,1,0:T(8,128)(2,1)} %get-tuple-element.121), channel_id=1, source_target_pairs={{0,2},{2,4},{4,6},{6,0},{1,3},{3,5},{5,7},{7,1},{8,10},{10,12},{12... | collective-permute-start | bytes 786440 | tf_op jit(solution)/shard_map/ppermute | solution.py:64
  573.1 11.0 %collective-permute-start.28 = (bf16[4,32,1024]{2,1,0:T(8,128)(2,1)}, bf16[4,32,1024]{2,1,0:T(8,128)(2,1)S(1)}, u32[]{:S(2)}, u32[]{:S(2)}) collective-permute-start(bf16[4,32,1024]{2,1,0:T(8,128)(2,1)} %get-tuple-element.123), channel_id=1, source_target_pairs={{0,6},{2,0},{4,2},{6,4},{1,7},{3,1},{5,3},{7,5},{8,14},{10,8},{12,... | collective-permute-start | bytes 786440 | tf_op jit(solution)/shard_map/ppermute | solution.py:64
  575.7 8.8 %collective-permute-start.29 = (bf16[4,32,1024]{2,1,0:T(8,128)(2,1)}, bf16[4,32,1024]{2,1,0:T(8,128)(2,1)S(1)}, u32[]{:S(2)}, u32[]{:S(2)}) collective-permute-start(bf16[4,32,1024]{2,1,0:T(8,128)(2,1)} %get-tuple-element.122), channel_id=1, source_target_pairs={{0,4},{2,6},{4,0},{6,2},{1,5},{3,7},{5,1},{7,3},{8,12},{10,14},{12... | collective-permute-start | bytes 786440 | tf_op jit(solution)/shard_map/ppermute | solution.py:64
  575.9 10.7 %collective-permute-start.39 = (bf16[4,32,1024]{2,1,0:T(8,128)(2,1)}, bf16[4,32,1024]{2,1,0:T(8,128)(2,1)S(1)}, u32[]{:S(2)}, u32[]{:S(2)}) collective-permute-start(bf16[4,32,1024]{2,1,0:T(8,128)(2,1)} %get-tuple-element.128), channel_id=1, source_target_pairs={{0,32},{32,64},{64,96},{96,0},{1,33},{33,65},{65,97},{97,1},{2,34}... | collective-permute-start | bytes 786440 | tf_op jit(solution)/shard_map/ppermute | solution.py:64
  577.8 11.6 %collective-permute-start.40 = (bf16[4,32,1024]{2,1,0:T(8,128)(2,1)}, bf16[4,32,1024]{2,1,0:T(8,128)(2,1)S(1)}, u32[]{:S(2)}, u32[]{:S(2)}) collective-permute-start(bf16[4,32,1024]{2,1,0:T(8,128)(2,1)} %get-tuple-element.130), channel_id=1, source_target_pairs={{0,96},{32,0},{64,32},{96,64},{1,97},{33,1},{65,33},{97,65},{2,98}... | collective-permute-start | bytes 786440 | tf_op jit(solution)/shard_map/ppermute | solution.py:64
  584.0 8.3 %collective-permute-start.41 = (bf16[4,32,1024]{2,1,0:T(8,128)(2,1)S(1)}, bf16[4,32,1024]{2,1,0:T(8,128)(2,1)S(1)}, u32[]{:S(2)}, u32[]{:S(2)}) collective-permute-start(bf16[4,32,1024]{2,1,0:T(8,128)(2,1)S(1)} %get-tuple-element.129), channel_id=1, source_target_pairs={{0,64},{32,96},{64,0},{96,32},{1,65},{33,97},{65,1},{97,33},{2,66}... | collective-permute-start | bytes 786440 | tf_op jit(solution)/shard_map/ppermute | solution.py:64
  584.5 9.3 %collective-permute-start.18 = (bf16[32,1024]{1,0:T(8,128)(2,1)S(1)}, bf16[32,1024]{1,0:T(8,128)(2,1)S(1)}, u32[]{:S(2)}, u32[]{:S(2)}) collective-permute-start(bf16[32,1024]{1,0:T(8,128)(2,1)S(1)} %get-tuple-element.152), channel_id=1, source_target_pairs={{0,2},{2,4},{4,6},{6,0},{1,3},{3,5},{5,7},{7,1},{8,10},{10,12},{12... | collective-permute-start | bytes 196616 | tf_op jit(solution)/shard_map/ppermute | solution.py:64
  586.5 9.9 %collective-permute-start.19 = (bf16[32,1024]{1,0:T(8,128)(2,1)S(1)}, bf16[32,1024]{1,0:T(8,128)(2,1)S(1)}, u32[]{:S(2)}, u32[]{:S(2)}) collective-permute-start(bf16[32,1024]{1,0:T(8,128)(2,1)S(1)} %get-tuple-element.154), channel_id=1, source_target_pairs={{0,6},{2,0},{4,2},{6,4},{1,7},{3,1},{5,3},{7,5},{8,14},{10,8},{12,... | collective-permute-start | bytes 196616 | tf_op jit(solution)/shard_map/ppermute | solution.py:64
  589.3 8.6 %collective-permute-start.20 = (bf16[32,1024]{1,0:T(8,128)(2,1)S(1)}, bf16[32,1024]{1,0:T(8,128)(2,1)S(1)}, u32[]{:S(2)}, u32[]{:S(2)}) collective-permute-start(bf16[32,1024]{1,0:T(8,128)(2,1)S(1)} %get-tuple-element.153), channel_id=1, source_target_pairs={{0,4},{2,6},{4,0},{6,2},{1,5},{3,7},{5,1},{7,3},{8,12},{10,14},{12... | collective-permute-start | bytes 196616 | tf_op jit(solution)/shard_map/ppermute | solution.py:64
  592.3 6.5 %collective-permute-start.30 = (bf16[32,1024]{1,0:T(8,128)(2,1)S(1)}, bf16[32,1024]{1,0:T(8,128)(2,1)S(1)}, u32[]{:S(2)}, u32[]{:S(2)}) collective-permute-start(bf16[32,1024]{1,0:T(8,128)(2,1)S(1)} %get-tuple-element.155), channel_id=1, source_target_pairs={{0,32},{32,64},{64,96},{96,0},{1,33},{33,65},{65,97},{97,1},{2,34}... | collective-permute-start | bytes 196616 | tf_op jit(solution)/shard_map/ppermute | solution.py:64
  593.8 7.5 %collective-permute-start.31 = (bf16[32,1024]{1,0:T(8,128)(2,1)S(1)}, bf16[32,1024]{1,0:T(8,128)(2,1)S(1)}, u32[]{:S(2)}, u32[]{:S(2)}) collective-permute-start(bf16[32,1024]{1,0:T(8,128)(2,1)S(1)} %get-tuple-element.157), channel_id=1, source_target_pairs={{0,96},{32,0},{64,32},{96,64},{1,97},{33,1},{65,33},{97,65},{2,98}... | collective-permute-start | bytes 196616 | tf_op jit(solution)/shard_map/ppermute | solution.py:64
  (125 other events, 1038.7 us)
